TPU v7x, 256 devices: a whole 4x4x8 slice. The times are simulated.
256 devices in a mesh: dp: 32 (over x, z_hi, core), ctx: 8 (over z_lo, y).
Axes of the slice: x: 4, y: 4, z: 8 (z_hi: 4, z_lo: 2; z = z_hi * 2 + z_lo), core: 2. Of those that a mesh axis runs over, the one named last changes fastest.
Arguments:
- hidden_in: bfloat16 [32, 1024, 2688], P('dp', 'ctx'), may hold values from -0.08984375 to 0.08984375
- queries: bfloat16 [32, 1024, 2048], P('dp', 'ctx'), may hold values from -60 to 60
- key_states: bfloat16 [32, 1024, 1024], P('dp', 'ctx'), may hold values from -4 to 4
- value_states: bfloat16 [32, 1024, 1024], P('dp', 'ctx'), may hold values from -6 to 6
- out_grad: bfloat16 [32, 1024, 2048], P('dp', 'ctx'), may hold values from -48 to 48
- segment_ids: int32 [32, 1024], P('dp', 'ctx'), may hold values from 0 to 3, never falling along the last dimension, each value on 1 to 512 neighbouring positions
Outputs:
- query_grad: bfloat16 [32, 1024, 2048], P('dp', 'ctx')
- key_grad: bfloat16 [32, 1024, 1024], P('dp', 'ctx')
- value_grad: bfloat16 [32, 1024, 1024], P('dp', 'ctx')
- weight_grad: float32 [2688, 2048], P('dp', 'ctx')
Inputs may be any that keep to these rules, and one draw needn't show every extreme that they name: `segment_ids`: documents of a trace are numbered in order of position.
All inputs are finite; a program needn't handle non-finite values.
Results may differ from a plain program's by a relative error of at most 0.0096.
Values may be sent and summed in bfloat16 or wider, within the bound.
A program may use at most 128 MiB of HBM per device.

v0:
```python
from functools import partial

import jax
import jax.numpy as jnp
from jax import lax
from jax.sharding import PartitionSpec as P

HD = 128
WIN = 1024


SCORE_FLOOR = -1e30


def shifted(value, axis, steps):
    count = lax.axis_size(axis)
    leading, last = (max(0, -steps), min(count, count - steps))
    return lax.ppermute(value, axis, [(source, source + steps) for source in range(leading, last)])


def head_grads(allowed, score_scale, operands):
    query_head, key_head, value_head, grad_head = operands
    scores = (
        jnp.einsum("igd,jd->gij", query_head, key_head, preferred_element_type=jnp.float32)
        * score_scale
    )
    scores = jnp.where(allowed[None], scores, SCORE_FLOOR)
    row_peak = jnp.max(scores, axis=2, keepdims=True)
    weights = jnp.where(allowed[None], jnp.exp(scores - row_peak), 0.0)
    probs_full = weights / jnp.sum(weights, axis=2, keepdims=True)
    probs_low = probs_full.astype(jnp.bfloat16)
    attn_out = jnp.einsum("gij,jd->gid", probs_low, value_head, preferred_element_type=jnp.float32)
    row_delta = jnp.einsum("igd,gid->gi", grad_head.astype(jnp.float32), attn_out)
    dprobs = jnp.einsum("igd,jd->gij", grad_head, value_head, preferred_element_type=jnp.float32)
    dscores = (probs_full * (dprobs - row_delta[:, :, None])).astype(jnp.bfloat16)
    query_part = (
        jnp.einsum("gij,jd->igd", dscores, key_head, preferred_element_type=jnp.float32)
        * score_scale
    ).astype(jnp.bfloat16)
    key_part = (
        jnp.einsum("gij,igd->jd", dscores, query_head, preferred_element_type=jnp.float32)
        * score_scale
    ).astype(jnp.bfloat16)
    value_part = jnp.einsum(
        "gij,igd->jd", probs_low, grad_head, preferred_element_type=jnp.float32
    ).astype(jnp.bfloat16)
    return (query_part, key_part, value_part)


def attend(allowed, score_scale, heads_in):
    query_heads, key_heads, value_heads, grad_heads = heads_in
    results = lax.map(
        partial(head_grads, allowed, score_scale), (query_heads, key_heads, value_heads, grad_heads)
    )
    return (results[0], results[1], results[2])


def local(hidden_in, queries, key_states, value_states, out_grad, segment_ids):
    tok_rows = queries.shape[1]
    key_width = key_states.shape[2]
    query_width = queries.shape[2]
    kv_heads = key_width // HD
    group_size = query_width // key_width
    score_scale = HD ** (-0.5)
    ctx_count = lax.axis_size("ctx")
    hop_count = min(WIN // tok_rows, ctx_count - 1)
    rim_span = hop_count * tok_rows
    ctx_place = lax.axis_index("ctx")
    own_keys = key_states[0]
    own_values = value_states[0]
    own_segs = segment_ids[0].astype(jnp.bfloat16)
    fetched = [
        shifted((own_keys, own_values, own_segs), "ctx", hop_index)
        for hop_index in range(hop_count, 0, -1)
    ]
    key_window = jnp.concatenate([fetched_item[0] for fetched_item in fetched] + [own_keys], axis=0)
    value_window = jnp.concatenate(
        [fetched_item[1] for fetched_item in fetched] + [own_values], axis=0
    )
    seg_window = jnp.concatenate([fetched_item[2] for fetched_item in fetched] + [own_segs], axis=0)
    seg_float = seg_window.astype(jnp.float32)
    query_segs = own_segs.astype(jnp.float32)
    query_pos = ctx_place * tok_rows + jnp.arange(tok_rows, dtype=jnp.int32)
    key_pos = ctx_place * tok_rows - rim_span + jnp.arange(tok_rows + rim_span, dtype=jnp.int32)
    distance = query_pos[:, None] - key_pos[None, :]
    allowed = (
        (key_pos[None, :] >= 0)
        & (distance >= 0)
        & (distance < WIN)
        & (query_segs[:, None] == seg_float[None, :])
    )
    query_heads = queries[0].reshape(tok_rows, kv_heads, group_size, HD).transpose(1, 0, 2, 3)
    grad_heads = out_grad[0].reshape(tok_rows, kv_heads, group_size, HD).transpose(1, 0, 2, 3)
    key_heads = key_window.reshape(-1, kv_heads, HD).transpose(1, 0, 2)
    value_heads = value_window.reshape(-1, kv_heads, HD).transpose(1, 0, 2)
    heads_in = (query_heads, key_heads, value_heads, grad_heads)
    query_part, key_part, value_part = attend(allowed, score_scale, heads_in)
    query_grad = query_part.transpose(1, 0, 2, 3).reshape(tok_rows, query_width)
    key_rows = key_part.transpose(1, 0, 2).reshape(-1, key_width)
    value_rows = value_part.transpose(1, 0, 2).reshape(-1, key_width)
    key_total = key_rows[rim_span:].astype(jnp.float32)
    value_total = value_rows[rim_span:].astype(jnp.float32)
    for hop_index in range(1, hop_count + 1):
        lower_row = rim_span - hop_index * tok_rows
        returned = shifted(
            (
                key_rows[lower_row : lower_row + tok_rows],
                value_rows[lower_row : lower_row + tok_rows],
            ),
            "ctx",
            -hop_index,
        )
        key_total = key_total + returned[0].astype(jnp.float32)
        value_total = value_total + returned[1].astype(jnp.float32)
    key_grad = key_total.astype(jnp.bfloat16)
    value_grad = value_total.astype(jnp.bfloat16)
    features = hidden_in[0]
    both_grads = jnp.concatenate([key_grad, value_grad], axis=1)
    contract_rows = (((0,), (0,)), ((), ()))
    column_block = lax.all_to_all(both_grads, "ctx", split_axis=1, concat_axis=0, tiled=True)
    trace_term = lax.dot_general(
        lax.all_gather(features, "ctx", axis=0, tiled=True),
        column_block,
        contract_rows,
        preferred_element_type=jnp.float32,
    )
    weight_grad = lax.psum_scatter(trace_term, "dp", scatter_dimension=0, tiled=True)
    return (query_grad[None], key_grad[None], value_grad[None], weight_grad)


def solution(mesh):
    placed = (
        P("dp", "ctx", None),
        P("dp", "ctx", None),
        P("dp", "ctx", None),
        P("dp", "ctx", None),
        P("dp", "ctx", None),
        P("dp", "ctx"),
    )
    return jax.shard_map(
        local,
        mesh=mesh,
        in_specs=placed,
        out_specs=(
            P("dp", "ctx", None),
            P("dp", "ctx", None),
            P("dp", "ctx", None),
            P("dp", "ctx"),
        ),
        check_vma=False,
    )
```

profile of v0, /device:TPU:1, one launch (start us, length us, event | category | flops | bytes accessed | tf_op | source)
XLA Modules:
  0.0 626.4 jit_solution(4404339890466291946)
XLA Ops:
  7.9 6.8 %collective-permute-start.7 = (bf16[128]{0:T(256)(128)(2,1)S(1)}, bf16[128]{0:T(256)(128)(2,1)S(1)}, u32[]{:S(2)}, u32[]{:S(2)}) collective-permute-start(bf16[128]{0:T(256)(128)(2,1)S(1)} %get-tuple-element.189), channel_id=1, source_target_pairs={{0,7},{8,15},{16,23},{24,31},{32,39},{40,47},{48,55},{56,63},{64,7... | collective-permute-start | bytes 776 | tf_op jit(solution)/shard_map/ppermute | solution.py:18
  17.2 2.0 collective-permute-start
  21.6 2.0 collective-permute-start.14
  29.2 9.9 %collective-permute-done.9 = bf16[128]{0:T(256)(128)(2,1)S(1)} collective-permute-done((bf16[128]{0:T(256)(128)(2,1)S(1)}, bf16[128]{0:T(256)(128)(2,1)S(1)}, u32[]{:S(2)}, u32[]{:S(2)}) %collective-permute-start.9) | collective-permute-done | bytes 288 | tf_op jit(solution)/shard_map/ppermute | solution.py:18
  40.6 7.1 %collective-permute-start.12 = (bf16[128]{0:T(256)(128)(2,1)S(1)}, bf16[128]{0:T(256)(128)(2,1)S(1)}, u32[]{:S(2)}, u32[]{:S(2)}) collective-permute-start(bf16[128]{0:T(256)(128)(2,1)S(1)} %get-tuple-element.189), channel_id=1, source_target_pairs={{0,2},{1,3},{2,4},{3,5},{4,6},{5,7},{8,10},{9,11},{10,12},{11,13},... | collective-permute-start | bytes 776 | tf_op jit(solution)/shard_map/ppermute | solution.py:18
  49.5 3.3 collective-permute-start.2
  53.0 2.1 collective-permute-start.3
  58.0 2.6 collective-permute-start.5
  61.6 1.9 collective-permute-start.6
  66.0 7.1 %collective-permute-done.3 = bf16[128,1024]{0,1:T(8,128)(2,1)} collective-permute-done((bf16[128,1024]{0,1:T(8,128)(2,1)S(1)}, bf16[128,1024]{0,1:T(8,128)(2,1)}, u32[]{:S(2)}, u32[]{:S(2)}) %collective-permute-start.3) | collective-permute-done | bytes 262176 | tf_op jit(solution)/shard_map/ppermute | solution.py:18
  75.4 2.9 collective-permute-done.4
  78.4 11.4 %collective-permute-start.17 = (bf16[128,1024]{0,1:T(8,128)(2,1)S(1)}, bf16[128,1024]{0,1:T(8,128)(2,1)S(1)}, u32[]{:S(2)}, u32[]{:S(2)}) collective-permute-start(bf16[128,1024]{0,1:T(8,128)(2,1)S(1)} %bitcast.281), channel_id=1, source_target_pairs={{0,4},{1,5},{2,6},{3,7},{8,12},{9,13},{10,14},{11,15},{16,20},{17,... | collective-permute-start | bytes 786440 | tf_op jit(solution)/shard_map/ppermute | solution.py:18
  89.9 5.9 collective-permute-start.18
  97.4 4.9 collective-permute-start.20
  102.5 4.3 collective-permute-done.17
  107.1 6.8 %collective-permute-done.20 = bf16[128,1024]{0,1:T(8,128)(2,1)S(1)} collective-permute-done((bf16[128,1024]{0,1:T(8,128)(2,1)S(1)}, bf16[128,1024]{0,1:T(8,128)(2,1)S(1)}, u32[]{:S(2)}, u32[]{:S(2)}) %collective-permute-start.20) | collective-permute-done | bytes 262176 | tf_op jit(solution)/shard_map/ppermute | solution.py:18
  115.5 104.0 %while.15 = (s32[]{:T(128)}, bf16[8,128,2,128]{1,3,2,0:T(8,128)(2,1)}, bf16[8,1024,128]{2,1,0:T(8,128)(2,1)S(1)}, bf16[8,1024,128]{2,1,0:T(8,128)(2,1)}, bf16[8,...) while((s32[]{:T(128)}, ...), condition=%wide.region_3.4_spmd.clone, body=%wide.region_0.3_spmd.clone.sunk | while | flops 543853824 | bytes 7495305 | solution.py:52
  116.4 2.6 fusion.148
  119.1 2.2 fusion.149
  124.1 2.5 fusion.153
  126.7 1.8 fusion.151
  129.4 2.6 fusion.148
  132.1 2.2 fusion.149
  137.1 2.5 fusion.153
  139.7 1.8 fusion.151
  142.4 2.6 fusion.148
  145.1 2.2 fusion.149
  150.1 2.5 fusion.153
  152.7 1.8 fusion.151
  155.4 2.6 fusion.148
  158.1 2.2 fusion.149
  163.1 2.6 fusion.153
  165.7 1.8 fusion.151
  168.4 2.6 fusion.148
  171.1 2.2 fusion.149
  176.2 2.6 fusion.153
  178.7 1.8 fusion.151
  181.4 2.6 fusion.148
  184.1 2.2 fusion.149
  189.2 2.5 fusion.153
  191.7 1.8 fusion.151
  194.4 2.6 fusion.148
  197.1 2.2 fusion.149
  202.2 2.5 fusion.153
  204.7 1.8 fusion.151
  207.4 2.6 fusion.148
  210.1 2.2 fusion.149
  215.2 2.5 fusion.153
  217.7 1.8 fusion.151
  219.5 2.6 fusion.103
  225.3 1.8 copy.118
  239.6 1.9 copy.109
  245.9 10.7 %collective-permute-done.30 = bf16[128,1024]{0,1:T(8,128)(2,1)} collective-permute-done((bf16[128,1024]{0,1:T(8,128)(2,1)}, bf16[128,1024]{0,1:T(8,128)(2,1)}, u32[]{:S(2)}, u32[]{:S(2)}) %collective-permute-start.30) | collective-permute-done | bytes 262176 | tf_op jit(solution)/shard_map/ppermute | solution.py:18
  257.9 10.9 %collective-permute-done.31 = bf16[128,1024]{0,1:T(8,128)(2,1)} collective-permute-done((bf16[128,1024]{0,1:T(8,128)(2,1)}, bf16[128,1024]{0,1:T(8,128)(2,1)}, u32[]{:S(2)}, u32[]{:S(2)}) %collective-permute-start.31) | collective-permute-done | bytes 262176 | tf_op jit(solution)/shard_map/ppermute | solution.py:18
  275.0 4.6 collective-permute-done.33
  280.9 3.4 collective-permute-done.34
  286.8 4.4 collective-permute-done.22
  294.3 2.8 collective-permute-done.23
  297.1 2.4 collective-permute-done.25
  299.4 1.9 collective-permute-done.26
  301.4 8.7 %collective-permute-done.27 = bf16[128,1024]{0,1:T(8,128)(2,1)S(1)} collective-permute-done((bf16[128,1024]{0,1:T(8,128)(2,1)S(1)}, bf16[128,1024]{0,1:T(8,128)(2,1)S(1)}, u32[]{:S(2)}, u32[]{:S(2)}) %collective-permute-start.27) | collective-permute-done | bytes 262176 | tf_op jit(solution)/shard_map/ppermute | solution.py:18
  310.3 10.0 %all_to_all.19 = bf16[128,8,256]{0,2,1:T(8,128)(2,1)S(1)} all-to-all(bf16[128,8,256]{0,2,1:T(8,128)(2,1)S(1)} %bitcast.275), channel_id=1, replica_groups=mesh['dp'=32,'ctx'=8] {'ctx'}, dimensions={1} | all-to-all | bytes 1048576 | tf_op jit(solution)/shard_map/all_to_all | solution.py:120
  320.6 5.8 fusion.80
  331.1 286.7 %all-reduce.3.cloned.1.call-done = f32[2688,256]{0,1:T(8,128)} async-done(((f32[2688,256]{0,1:T(8,128)}), f32[2688,256]{0,1:T(8,128)}) %all-reduce.3.cloned.1.call-update) | async-done | bytes 2752528
  (170 shorter events, 97.9 us)
Async XLA Ops:
  7.2 16.6 %copy-start.5 = (bf16[1,128,2048]{2,1,0:T(8,128)(2,1)S(1)}, bf16[1,128,2048]{2,1,0:T(8,128)(2,1)}, u32[]{:S(2)}) copy-start(bf16[1,128,2048]{2,1,0:T(8,128)(2,1)} %param.9) | copy-start | bytes 1572868
  7.2 313.4 %all-gather.3.cloned.1.call-start = ((), (), s32[]{:S(2)}) async-start(), calls=%async_computation.1 | async-start | bytes 6193152 | tf_op jit(solution)/shard_map/all_gather | solution.py:122
  7.9 18.2 %collective-permute-start.7 = (bf16[128]{0:T(256)(128)(2,1)S(1)}, bf16[128]{0:T(256)(128)(2,1)S(1)}, u32[]{:S(2)}, u32[]{:S(2)}) collective-permute-start(bf16[128]{0:T(256)(128)(2,1)S(1)} %get-tuple-element.189), channel_id=1, source_target_pairs={{0,7},{8,15},{16,23},{24,31},{32,39},{40,47},{48,55},{56,63},{64,7... | collective-permute-start | bytes 776 | tf_op jit(solution)/shard_map/ppermute | solution.py:18
  14.7 12.9 %collective-permute-start.8 = (bf16[128]{0:T(256)(128)(2,1)S(1)}, bf16[128]{0:T(256)(128)(2,1)S(1)}, u32[]{:S(2)}, u32[]{:S(2)}) collective-permute-start(bf16[128]{0:T(256)(128)(2,1)S(1)} %get-tuple-element.189), channel_id=1, source_target_pairs={{0,6},{1,7},{8,14},{9,15},{16,22},{17,23},{24,30},{25,31},{32,38},... | collective-permute-start | bytes 776 | tf_op jit(solution)/shard_map/ppermute | solution.py:18
  17.2 38.2 %collective-permute-start = (bf16[128,1024]{0,1:T(8,128)(2,1)S(1)}, bf16[128,1024]{0,1:T(8,128)(2,1)}, u32[]{:S(2)}, u32[]{:S(2)}) collective-permute-start(bf16[128,1024]{0,1:T(8,128)(2,1)S(1)} %bitcast.286), channel_id=1, source_target_pairs={{0,7},{8,15},{16,23},{24,31},{32,39},{40,47},{48,55},{56,63},{64,7... | collective-permute-start | bytes 786440 | tf_op jit(solution)/shard_map/ppermute | solution.py:18
  19.2 42.4 %collective-permute-start.1 = (bf16[128,1024]{0,1:T(8,128)(2,1)S(1)}, bf16[128,1024]{0,1:T(8,128)(2,1)S(1)}, u32[]{:S(2)}, u32[]{:S(2)}) collective-permute-start(bf16[128,1024]{0,1:T(8,128)(2,1)S(1)} %bitcast.287), channel_id=1, source_target_pairs={{0,6},{1,7},{8,14},{9,15},{16,22},{17,23},{24,30},{25,31},{32,38},... | collective-permute-start | bytes 786440 | tf_op jit(solution)/shard_map/ppermute | solution.py:18
  21.6 36.4 %collective-permute-start.14 = (bf16[128,1024]{0,1:T(8,128)(2,1)S(1)}, bf16[128,1024]{0,1:T(8,128)(2,1)}, u32[]{:S(2)}, u32[]{:S(2)}) collective-permute-start(bf16[128,1024]{0,1:T(8,128)(2,1)S(1)} %bitcast.278), channel_id=1, source_target_pairs={{0,7},{8,15},{16,23},{24,31},{32,39},{40,47},{48,55},{56,63},{64,7... | collective-permute-start | bytes 786440 | tf_op jit(solution)/shard_map/ppermute | solution.py:18
  23.6 594.2 %all-reduce.3.cloned.1.call-start = ((), (), s32[]{:S(2)}) async-start(), calls=%async_computation.2 | async-start | bytes 5505024
  26.1 13.0 %collective-permute-start.9 = (bf16[128]{0:T(256)(128)(2,1)S(1)}, bf16[128]{0:T(256)(128)(2,1)S(1)}, u32[]{:S(2)}, u32[]{:S(2)}) collective-permute-start(bf16[128]{0:T(256)(128)(2,1)S(1)} %get-tuple-element.189), channel_id=1, source_target_pairs={{0,5},{1,6},{2,7},{8,13},{9,14},{10,15},{16,21},{17,22},{18,23},{2... | collective-permute-start | bytes 776 | tf_op jit(solution)/shard_map/ppermute | solution.py:18
  27.6 13.0 %collective-permute-start.10 = (bf16[128]{0:T(256)(128)(2,1)S(1)}, bf16[128]{0:T(256)(128)(2,1)S(1)}, u32[]{:S(2)}, u32[]{:S(2)}) collective-permute-start(bf16[128]{0:T(256)(128)(2,1)S(1)} %get-tuple-element.189), channel_id=1, source_target_pairs={{0,4},{1,5},{2,6},{3,7},{8,12},{9,13},{10,14},{11,15},{16,20},{17,... | collective-permute-start | bytes 776 | tf_op jit(solution)/shard_map/ppermute | solution.py:18
  39.1 8.9 %collective-permute-start.11 = (bf16[128]{0:T(256)(128)(2,1)S(1)}, bf16[128]{0:T(256)(128)(2,1)S(1)}, u32[]{:S(2)}, u32[]{:S(2)}) collective-permute-start(bf16[128]{0:T(256)(128)(2,1)S(1)} %get-tuple-element.189), channel_id=1, source_target_pairs={{0,3},{1,4},{2,5},{3,6},{4,7},{8,11},{9,12},{10,13},{11,14},{12,15... | collective-permute-start | bytes 776 | tf_op jit(solution)/shard_map/ppermute | solution.py:18
  40.6 8.9 %collective-permute-start.12 = (bf16[128]{0:T(256)(128)(2,1)S(1)}, bf16[128]{0:T(256)(128)(2,1)S(1)}, u32[]{:S(2)}, u32[]{:S(2)}) collective-permute-start(bf16[128]{0:T(256)(128)(2,1)S(1)} %get-tuple-element.189), channel_id=1, source_target_pairs={{0,2},{1,3},{2,4},{3,5},{4,6},{5,7},{8,10},{9,11},{10,12},{11,13},... | collective-permute-start | bytes 776 | tf_op jit(solution)/shard_map/ppermute | solution.py:18
  48.0 5.0 collective-permute-start.13
  49.5 14.1 %collective-permute-start.2 = (bf16[128,1024]{0,1:T(8,128)(2,1)S(1)}, bf16[128,1024]{0,1:T(8,128)(2,1)}, u32[]{:S(2)}, u32[]{:S(2)}) collective-permute-start(bf16[128,1024]{0,1:T(8,128)(2,1)S(1)} %bitcast.288), channel_id=1, source_target_pairs={{0,5},{1,6},{2,7},{8,13},{9,14},{10,15},{16,21},{17,22},{18,23},{2... | collective-permute-start | bytes 786440 | tf_op jit(solution)/shard_map/ppermute | solution.py:18
  53.0 20.1 %collective-permute-start.3 = (bf16[128,1024]{0,1:T(8,128)(2,1)S(1)}, bf16[128,1024]{0,1:T(8,128)(2,1)}, u32[]{:S(2)}, u32[]{:S(2)}) collective-permute-start(bf16[128,1024]{0,1:T(8,128)(2,1)S(1)} %bitcast.289), channel_id=1, source_target_pairs={{0,4},{1,5},{2,6},{3,7},{8,12},{9,13},{10,14},{11,15},{16,20},{17,... | collective-permute-start | bytes 786440 | tf_op jit(solution)/shard_map/ppermute | solution.py:18
  55.4 23.0 %collective-permute-start.4 = (bf16[128,1024]{0,1:T(8,128)(2,1)S(1)}, bf16[128,1024]{0,1:T(8,128)(2,1)S(1)}, u32[]{:S(2)}, u32[]{:S(2)}) collective-permute-start(bf16[128,1024]{0,1:T(8,128)(2,1)S(1)} %bitcast.290), channel_id=1, source_target_pairs={{0,3},{1,4},{2,5},{3,6},{4,7},{8,11},{9,12},{10,13},{11,14},{12,15... | collective-permute-start | bytes 786440 | tf_op jit(solution)/shard_map/ppermute | solution.py:18
  58.0 31.8 %collective-permute-start.5 = (bf16[128,1024]{0,1:T(8,128)(2,1)S(1)}, bf16[128,1024]{0,1:T(8,128)(2,1)S(1)}, u32[]{:S(2)}, u32[]{:S(2)}) collective-permute-start(bf16[128,1024]{0,1:T(8,128)(2,1)S(1)} %bitcast.291), channel_id=1, source_target_pairs={{0,2},{1,3},{2,4},{3,5},{4,6},{5,7},{8,10},{9,11},{10,12},{11,13},... | collective-permute-start | bytes 786440 | tf_op jit(solution)/shard_map/ppermute | solution.py:18
  61.6 34.3 %collective-permute-start.6 = (bf16[128,1024]{0,1:T(8,128)(2,1)S(1)}, bf16[128,1024]{0,1:T(8,128)(2,1)S(1)}, u32[]{:S(2)}, u32[]{:S(2)}) collective-permute-start(bf16[128,1024]{0,1:T(8,128)(2,1)S(1)} %bitcast.292), channel_id=1, source_target_pairs={{0,1},{1,2},{2,3},{3,4},{4,5},{5,6},{6,7},{8,9},{9,10},{10,11},{11... | collective-permute-start | bytes 786440 | tf_op jit(solution)/shard_map/ppermute | solution.py:18
  63.6 33.8 %collective-permute-start.15 = (bf16[128,1024]{0,1:T(8,128)(2,1)S(1)}, bf16[128,1024]{0,1:T(8,128)(2,1)S(1)}, u32[]{:S(2)}, u32[]{:S(2)}) collective-permute-start(bf16[128,1024]{0,1:T(8,128)(2,1)S(1)} %bitcast.279), channel_id=1, source_target_pairs={{0,6},{1,7},{8,14},{9,15},{16,22},{17,23},{24,30},{25,31},{32,38},... | collective-permute-start | bytes 786440 | tf_op jit(solution)/shard_map/ppermute | solution.py:18
  73.1 29.3 %collective-permute-start.16 = (bf16[128,1024]{0,1:T(8,128)(2,1)S(1)}, bf16[128,1024]{0,1:T(8,128)(2,1)S(1)}, u32[]{:S(2)}, u32[]{:S(2)}) collective-permute-start(bf16[128,1024]{0,1:T(8,128)(2,1)S(1)} %bitcast.280), channel_id=1, source_target_pairs={{0,5},{1,6},{2,7},{8,13},{9,14},{10,15},{16,21},{17,22},{18,23},{2... | collective-permute-start | bytes 786440 | tf_op jit(solution)/shard_map/ppermute | solution.py:18
  78.4 28.4 %collective-permute-start.17 = (bf16[128,1024]{0,1:T(8,128)(2,1)S(1)}, bf16[128,1024]{0,1:T(8,128)(2,1)S(1)}, u32[]{:S(2)}, u32[]{:S(2)}) collective-permute-start(bf16[128,1024]{0,1:T(8,128)(2,1)S(1)} %bitcast.281), channel_id=1, source_target_pairs={{0,4},{1,5},{2,6},{3,7},{8,12},{9,13},{10,14},{11,15},{16,20},{17,... | collective-permute-start | bytes 786440 | tf_op jit(solution)/shard_map/ppermute | solution.py:18
  89.9 17.0 %collective-permute-start.18 = (bf16[128,1024]{0,1:T(8,128)(2,1)S(1)}, bf16[128,1024]{0,1:T(8,128)(2,1)S(1)}, u32[]{:S(2)}, u32[]{:S(2)}) collective-permute-start(bf16[128,1024]{0,1:T(8,128)(2,1)S(1)} %bitcast.282), channel_id=1, source_target_pairs={{0,3},{1,4},{2,5},{3,6},{4,7},{8,11},{9,12},{10,13},{11,14},{12,15... | collective-permute-start | bytes 786440 | tf_op jit(solution)/shard_map/ppermute | solution.py:18
  95.9 11.1 %collective-permute-start.19 = (bf16[128,1024]{0,1:T(8,128)(2,1)S(1)}, bf16[128,1024]{0,1:T(8,128)(2,1)S(1)}, u32[]{:S(2)}, u32[]{:S(2)}) collective-permute-start(bf16[128,1024]{0,1:T(8,128)(2,1)S(1)} %bitcast.283), channel_id=1, source_target_pairs={{0,2},{1,3},{2,4},{3,5},{4,6},{5,7},{8,10},{9,11},{10,12},{11,13},... | collective-permute-start | bytes 786440 | tf_op jit(solution)/shard_map/ppermute | solution.py:18
  97.4 16.7 %copy-start = (bf16[1024,8,128]{0,2,1:T(8,128)(2,1)}, bf16[1024,8,128]{0,2,1:T(8,128)(2,1)S(1)}, u32[]{:S(2)}) copy-start(bf16[1024,8,128]{0,2,1:T(8,128)(2,1)S(1)} %constant_dynamic-update-slice_fusion) | copy-start | bytes 6291460
  97.4 16.5 %collective-permute-start.20 = (bf16[128,1024]{0,1:T(8,128)(2,1)S(1)}, bf16[128,1024]{0,1:T(8,128)(2,1)S(1)}, u32[]{:S(2)}, u32[]{:S(2)}) collective-permute-start(bf16[128,1024]{0,1:T(8,128)(2,1)S(1)} %bitcast.284), channel_id=1, source_target_pairs={{0,1},{1,2},{2,3},{3,4},{4,5},{5,6},{6,7},{8,9},{9,10},{10,11},{11... | collective-permute-start | bytes 786440 | tf_op jit(solution)/shard_map/ppermute | solution.py:18
  114.1 1.4 copy-start.7
  224.0 19.3 %collective-permute-start.28 = (bf16[128,1024]{0,1:T(8,128)(2,1)}, bf16[128,1024]{0,1:T(8,128)(2,1)}, u32[]{:S(2)}, u32[]{:S(2)}) collective-permute-start(bf16[128,1024]{0,1:T(8,128)(2,1)} %bitcast.312), channel_id=1, source_target_pairs={{1,0},{2,1},{3,2},{4,3},{5,4},{6,5},{7,6},{9,8},{10,9},{11,10},{12... | collective-permute-start | bytes 786440 | tf_op jit(solution)/shard_map/ppermute | solution.py:18
  227.1 17.5 %collective-permute-start.29 = (bf16[128,1024]{0,1:T(8,128)(2,1)}, bf16[128,1024]{0,1:T(8,128)(2,1)}, u32[]{:S(2)}, u32[]{:S(2)}) collective-permute-start(bf16[128,1024]{0,1:T(8,128)(2,1)} %bitcast.311), channel_id=1, source_target_pairs={{2,0},{3,1},{4,2},{5,3},{6,4},{7,5},{10,8},{11,9},{12,10},{13,11},... | collective-permute-start | bytes 786440 | tf_op jit(solution)/shard_map/ppermute | solution.py:18
  230.2 26.4 %collective-permute-start.30 = (bf16[128,1024]{0,1:T(8,128)(2,1)}, bf16[128,1024]{0,1:T(8,128)(2,1)}, u32[]{:S(2)}, u32[]{:S(2)}) collective-permute-start(bf16[128,1024]{0,1:T(8,128)(2,1)} %bitcast.307), channel_id=1, source_target_pairs={{3,0},{4,1},{5,2},{6,3},{7,4},{11,8},{12,9},{13,10},{14,11},{15,12... | collective-permute-start | bytes 786440 | tf_op jit(solution)/shard_map/ppermute | solution.py:18
  233.3 35.5 %collective-permute-start.31 = (bf16[128,1024]{0,1:T(8,128)(2,1)}, bf16[128,1024]{0,1:T(8,128)(2,1)}, u32[]{:S(2)}, u32[]{:S(2)}) collective-permute-start(bf16[128,1024]{0,1:T(8,128)(2,1)} %bitcast.305), channel_id=1, source_target_pairs={{4,0},{5,1},{6,2},{7,3},{12,8},{13,9},{14,10},{15,11},{20,16},{21,... | collective-permute-start | bytes 786440 | tf_op jit(solution)/shard_map/ppermute | solution.py:18
  235.4 38.2 %collective-permute-start.32 = (bf16[128,1024]{0,1:T(8,128)(2,1)}, bf16[128,1024]{0,1:T(8,128)(2,1)}, u32[]{:S(2)}, u32[]{:S(2)}) collective-permute-start(bf16[128,1024]{0,1:T(8,128)(2,1)} %bitcast.298), channel_id=1, source_target_pairs={{5,0},{6,1},{7,2},{13,8},{14,9},{15,10},{21,16},{22,17},{23,18},{2... | collective-permute-start | bytes 786440 | tf_op jit(solution)/shard_map/ppermute | solution.py:18
  239.6 30.9 %copy-start.4 = (bf16[128,8,128]{2,0,1:T(8,128)(2,1)S(1)}, bf16[128,8,128]{2,0,1:T(8,128)(2,1)}, u32[]{:S(2)}) copy-start(bf16[128,8,128]{2,0,1:T(8,128)(2,1)} %get-tuple-element.185) | copy-start | bytes 786436
  239.6 31.8 %copy-start.3 = (bf16[128,8,128]{2,0,1:T(8,128)(2,1)S(1)}, bf16[128,8,128]{2,0,1:T(8,128)(2,1)}, u32[]{:S(2)}) copy-start(bf16[128,8,128]{2,0,1:T(8,128)(2,1)} %get-tuple-element.184) | copy-start | bytes 786436
  239.6 32.7 %copy-start.2 = (bf16[128,8,128]{2,0,1:T(8,128)(2,1)S(1)}, bf16[128,8,128]{2,0,1:T(8,128)(2,1)}, u32[]{:S(2)}) copy-start(bf16[128,8,128]{2,0,1:T(8,128)(2,1)} %get-tuple-element.183) | copy-start | bytes 786436
  239.6 33.5 %copy-start.1 = (bf16[128,8,128]{2,0,1:T(8,128)(2,1)S(1)}, bf16[128,8,128]{2,0,1:T(8,128)(2,1)}, u32[]{:S(2)}) copy-start(bf16[128,8,128]{2,0,1:T(8,128)(2,1)} %get-tuple-element.182) | copy-start | bytes 786436
  243.3 36.3 %collective-permute-start.33 = (bf16[128,1024]{0,1:T(8,128)(2,1)}, bf16[128,1024]{0,1:T(8,128)(2,1)}, u32[]{:S(2)}, u32[]{:S(2)}) collective-permute-start(bf16[128,1024]{0,1:T(8,128)(2,1)} %bitcast.297), channel_id=1, source_target_pairs={{6,0},{7,1},{14,8},{15,9},{22,16},{23,17},{30,24},{31,25},{38,32},... | collective-permute-start | bytes 786440 | tf_op jit(solution)/shard_map/ppermute | solution.py:18
  244.6 39.7 %collective-permute-start.34 = (bf16[128,1024]{0,1:T(8,128)(2,1)}, bf16[128,1024]{0,1:T(8,128)(2,1)}, u32[]{:S(2)}, u32[]{:S(2)}) collective-permute-start(bf16[128,1024]{0,1:T(8,128)(2,1)} %bitcast.296), channel_id=1, source_target_pairs={{7,0},{15,8},{23,16},{31,24},{39,32},{47,40},{55,48},{63,56},{71,6... | collective-permute-start | bytes 786440 | tf_op jit(solution)/shard_map/ppermute | solution.py:18
  256.6 28.9 %collective-permute-start.21 = (bf16[128,1024]{0,1:T(8,128)(2,1)}, bf16[128,1024]{0,1:T(8,128)(2,1)S(1)}, u32[]{:S(2)}, u32[]{:S(2)}) collective-permute-start(bf16[128,1024]{0,1:T(8,128)(2,1)} %bitcast.30), channel_id=1, source_target_pairs={{1,0},{2,1},{3,2},{4,3},{5,4},{6,5},{7,6},{9,8},{10,9},{11,10},{12... | collective-permute-start | bytes 786440 | tf_op jit(solution)/shard_map/ppermute | solution.py:18
  268.8 22.5 %collective-permute-start.22 = (bf16[128,1024]{0,1:T(8,128)(2,1)}, bf16[128,1024]{0,1:T(8,128)(2,1)S(1)}, u32[]{:S(2)}, u32[]{:S(2)}) collective-permute-start(bf16[128,1024]{0,1:T(8,128)(2,1)} %bitcast.31), channel_id=1, source_target_pairs={{2,0},{3,1},{4,2},{5,3},{6,4},{7,5},{10,8},{11,9},{12,10},{13,11},... | collective-permute-start | bytes 786440 | tf_op jit(solution)/shard_map/ppermute | solution.py:18
  273.7 23.4 %collective-permute-start.23 = (bf16[128,1024]{0,1:T(8,128)(2,1)}, bf16[128,1024]{0,1:T(8,128)(2,1)S(1)}, u32[]{:S(2)}, u32[]{:S(2)}) collective-permute-start(bf16[128,1024]{0,1:T(8,128)(2,1)} %bitcast.303), channel_id=1, source_target_pairs={{3,0},{4,1},{5,2},{6,3},{7,4},{11,8},{12,9},{13,10},{14,11},{15,12... | collective-permute-start | bytes 786440 | tf_op jit(solution)/shard_map/ppermute | solution.py:18
  279.6 17.5 %collective-permute-start.24 = (bf16[128,1024]{0,1:T(8,128)(2,1)}, bf16[128,1024]{0,1:T(8,128)(2,1)S(1)}, u32[]{:S(2)}, u32[]{:S(2)}) collective-permute-start(bf16[128,1024]{0,1:T(8,128)(2,1)} %bitcast.302), channel_id=1, source_target_pairs={{4,0},{5,1},{6,2},{7,3},{12,8},{13,9},{14,10},{15,11},{20,16},{21,... | collective-permute-start | bytes 786440 | tf_op jit(solution)/shard_map/ppermute | solution.py:18
  284.2 15.2 %collective-permute-start.25 = (bf16[128,1024]{0,1:T(8,128)(2,1)}, bf16[128,1024]{0,1:T(8,128)(2,1)S(1)}, u32[]{:S(2)}, u32[]{:S(2)}) collective-permute-start(bf16[128,1024]{0,1:T(8,128)(2,1)} %bitcast.301), channel_id=1, source_target_pairs={{5,0},{6,1},{7,2},{13,8},{14,9},{15,10},{21,16},{22,17},{23,18},{2... | collective-permute-start | bytes 786440 | tf_op jit(solution)/shard_map/ppermute | solution.py:18
  285.5 15.8 %collective-permute-start.26 = (bf16[128,1024]{0,1:T(8,128)(2,1)S(1)}, bf16[128,1024]{0,1:T(8,128)(2,1)S(1)}, u32[]{:S(2)}, u32[]{:S(2)}) collective-permute-start(bf16[128,1024]{0,1:T(8,128)(2,1)S(1)} %bitcast.300), channel_id=1, source_target_pairs={{6,0},{7,1},{14,8},{15,9},{22,16},{23,17},{30,24},{31,25},{38,32},... | collective-permute-start | bytes 786440 | tf_op jit(solution)/shard_map/ppermute | solution.py:18
  291.3 18.7 %collective-permute-start.27 = (bf16[128,1024]{0,1:T(8,128)(2,1)S(1)}, bf16[128,1024]{0,1:T(8,128)(2,1)S(1)}, u32[]{:S(2)}, u32[]{:S(2)}) collective-permute-start(bf16[128,1024]{0,1:T(8,128)(2,1)S(1)} %bitcast.299), channel_id=1, source_target_pairs={{7,0},{15,8},{23,16},{31,24},{39,32},{47,40},{55,48},{63,56},{71,6... | collective-permute-start | bytes 786440 | tf_op jit(solution)/shard_map/ppermute | solution.py:18
  326.5 0.7 copy-start.8
  326.5 1.9 copy-start.6
Sparse Core Ops, SparseCore 0:
  23.8 97.7 all-gather.2
  326.6 291.1 all-reduce.2
where the time goes:
time: 631 us; the launch traced here: 626 us
  waiting for transfers between devices  368 us (58%)
  matrix products  102 us (16%)
  starting transfers between devices  81.3 us (13%)
  local copies, waits for them, and re-layouts  36.5 us (6%)
  between operations  15.4 us (2%)
  other arithmetic  13.5 us (2%)
  blocking collectives  10 us (2%)
    unnamed x3, waiting for transfers between devices  287 us
    ppermute x35, starting transfers between devices, shifted(): lax.ppermute(value, axis, [(source, source + steps) for source in range(l...  81.2 us
    ppermute x35, waiting for transfers between devices, shifted(): lax.ppermute(value, axis, [(source, source + steps) for source in range(l...  81 us
    sub x8, matrix products, head_grads(): weights = jnp.where(allowed[None], jnp.exp(scores - row_peak), 0.0)  20.8 us
    dot_general x8, matrix products, head_grads(): jnp.einsum('gij,igd->jd', probs_low, grad_head, preferred_element_type=jn...  20.4 us
    dot_general x8, matrix products, head_grads(): jnp.einsum('gij,jd->gid', probs_low, value_head, preferred_element_type=j...  17.4 us
    unnamed x48, local copies, waits for them, and re-layouts  17.1 us
    dot_general x8, matrix products, head_grads(): jnp.einsum('gij,jd->igd', dscores, key_head, preferred_element_type=jnp.f...  14.5 us
  transfers between devices with their start and end apart: 37, of which 15 were waited for; matrix products, arithmetic and copies ran while one was open for 23% of the time, Pallas kernels for 0%

commit v1 on v0

v1 whole, which is shorter than its diff:
```python
import functools

import jax
import jax.numpy as jnp
from jax import lax
from jax.experimental import pallas as pl
from jax.experimental.pallas import tpu as pltpu
from jax.sharding import PartitionSpec as P

HD = 128
TOK = 128
CTX = 8
NY = 4
NX = 4
NZ = 4
NC = 2
SPAN = 4
FLOOR = -1e30
SCALE = HD ** (-0.5)
EXP2_SCALE = SCALE * 1.4426950408889634
MESH = pl.DeviceIdType.MESH
F32 = jnp.float32
BF16 = jnp.bfloat16
PEERS = ((1, 2), (0, 2), (1, 1), (1, 3), (0, 1), (0, 3), (1, 0))
NT = (((1,), (1,)), ((), ()))
TN = (((0,), (0,)), ((), ()))


def dot(lhs, rhs, dims=(((1,), (0,)), ((), ()))):
    return lax.dot_general(lhs, rhs, dims, preferred_element_type=F32)


def kernel(
    h, q, k, v, do, seg, dq_out, dk_out, dv_out, w_out,
    hv, qs, dos, ks, vs, segs, segc, dqs, g4, dka, dva, hs, hall,
    wown, csend, crecv, xsend, xrecv, tsum, zsend, zrecv,
    lsem, asend, arecv, osend, orecv, gsend, grecv, hsend, hrecv,
    csem, crsem, xsem, xrsem, zsem, zrsem,
):
    feats = h.shape[1]
    half = feats // 2
    xrows = half // NX
    frows = w_out.shape[0]
    zrows = zsend.shape[1]
    dp = lax.axis_index("dp")
    ctx = lax.axis_index("ctx")
    x = dp // (NZ * NC)
    zh = (dp // NC) % NZ
    core = dp % NC
    zl = ctx // NY
    y = ctx % NY
    other = (zl + 1) % 2
    head = 2 * y + zl
    partner = other * NY + y

    def at(place, width):
        return pl.ds(pl.multiple_of(place * width, width), width)

    def place(nx, nz, nc, nl, ny):
        return ((nx * NZ + nz) * NC + nc, nl * NY + ny)

    def remote(src, dst, ssem, rsem, device):
        return pltpu.make_async_remote_copy(
            src_ref=src, dst_ref=dst, send_sem=ssem, recv_sem=rsem,
            device_id=device, device_id_type=MESH,
        )

    barrier = pltpu.get_barrier_semaphore()
    count = 0
    for dz in range(NZ):
        for dc in range(NC):
            for dl in range(2):
                if dz + dc + dl:
                    pl.semaphore_signal(
                        barrier, inc=1, device_id_type=MESH,
                        device_id=place(x, (zh + dz) % NZ, (core + dc) % NC, (zl + dl) % 2, y),
                    )
                    count += 1
    for dl in range(2):
        for dy in range(1, NY):
            pl.semaphore_signal(
                barrier, inc=1, device_id_type=MESH,
                device_id=place(x, zh, core, (zl + dl) % 2, (y + dy) % NY),
            )
            count += 1
    for dx in range(1, NX):
        pl.semaphore_signal(
            barrier, inc=1, device_id_type=MESH,
            device_id=place((x + dx) % NX, zh, core, zl, y),
        )
        count += 1

    own = at(ctx, TOK)
    local_in = [
        pltpu.make_async_copy(h, hv, lsem.at[0]),
        pltpu.make_async_copy(q.at[:, at(head, 2 * HD)], qs.at[own, :], lsem.at[1]),
        pltpu.make_async_copy(do.at[:, at(head, 2 * HD)], dos.at[own, :], lsem.at[2]),
        pltpu.make_async_copy(k.at[:, at(head, HD)], ks.at[own, :], lsem.at[3]),
        pltpu.make_async_copy(v.at[:, at(head, HD)], vs.at[own, :], lsem.at[4]),
        pltpu.make_async_copy(seg, segs.at[ctx], lsem.at[5]),
    ]
    for copy in local_in:
        copy.start()
    pl.semaphore_wait(barrier, count)

    def inputs_to(nl, ny, slot, sender):
        to_head = 2 * ny + nl
        target = (dp, nl * NY + ny)
        rows = at(sender, TOK)
        pairs = (
            (k.at[:, at(to_head, HD)], ks.at[rows, :]),
            (q.at[:, at(to_head, 2 * HD)], qs.at[rows, :]),
            (v.at[:, at(to_head, HD)], vs.at[rows, :]),
            (do.at[:, at(to_head, 2 * HD)], dos.at[rows, :]),
            (seg, segs.at[sender]),
        )
        return [
            remote(src, dst, asend.at[index, slot], arecv.at[index, sender], target)
            for index, (src, dst) in enumerate(pairs)
        ]

    input_copies = []
    for slot, (dl, dy) in enumerate(PEERS):
        input_copies += inputs_to((zl + dl) % 2, (y + dy) % NY, slot, ctx)
    for copy in input_copies:
        copy.start()

    local_in[0].wait()
    for tile in range(feats // 128):
        turned = jnp.transpose(hv[:, tile * 128 : (tile + 1) * 128])
        row = tile * 128
        while row < (tile + 1) * 128:
            block = row // xrows
            stop = min((block + 1) * xrows, (tile + 1) * 128)
            start = (block // 2) * xrows + row - block * xrows
            hs[block % 2, start : start + stop - row, :] = turned[
                row - tile * 128 : stop - tile * 128, :
            ]
            row = stop

    h_across = remote(
        hs.at[other], hall.at[:, own], hsend.at[0], hrecv.at[ctx], (dp, partner)
    )
    h_across.start()
    h_own = pltpu.make_async_copy(hs.at[zl], hall.at[:, own], lsem.at[6])
    h_own.start()
    h_copies = [
        remote(
            hs.at[zl], hall.at[:, own], hsend.at[dy], hrecv.at[ctx],
            (dp, zl * NY + (y + dy) % NY),
        )
        for dy in (2, 1, 3)
    ]
    theirs = at(partner, TOK)
    h_passed = [
        remote(
            hall.at[:, theirs], hall.at[:, theirs], hsend.at[NY - 1 + dy], hrecv.at[partner],
            (dp, zl * NY + (y + dy) % NY),
        )
        for dy in (2, 1, 3)
    ]
    h_from_partner = remote(
        hs.at[other], hall.at[:, theirs], hsend.at[0], hrecv.at[partner], (dp, partner)
    )

    for copy in local_in[1:]:
        copy.wait()

    def out_copy(index, src, dst, block):
        return (
            remote(src, dst, osend.at[index, block], orecv.at[index, ctx], (dp, block)),
            pltpu.make_async_copy(src, dst, osend.at[index, block]),
        )

    def out_sends(block):
        rows = pl.ds(block * TOK, TOK)
        return (
            out_copy(0, dqs.at[rows, :], dq_out.at[:, at(head, 2 * HD)], block),
            out_copy(1, g4.at[zl, rows, :], dk_out.at[:, at(head, HD)], block),
            out_copy(2, g4.at[2 + zl, rows, :], dv_out.at[:, at(head, HD)], block),
        )

    def start_out(index, block):
        far, near = out_sends(block)[index]

        @pl.when(ctx != block)
        def _():
            far.start()

        @pl.when(ctx == block)
        def _():
            near.start()

    def trade(block, mine):
        rows = pl.ds(block * TOK, TOK)
        which = zl if mine else other
        return [
            remote(
                g4.at[2 * kind + which, rows, :], g4.at[2 * kind + which, rows, :],
                gsend.at[kind, block], grecv.at[kind, block], (dp, partner),
            )
            for kind in range(2)
        ]

    def finish_keys(block):
        rows = slice(block * TOK, (block + 1) * TOK)
        g4[zl, rows, :] = (dka[rows, :] * SCALE).astype(BF16)
        g4[2 + zl, rows, :] = dva[rows, :].astype(BF16)
        for copy in trade(block, True):
            copy.start()
        start_out(1, block)
        start_out(2, block)

    key_iota = lax.broadcasted_iota(jnp.int32, (TOK, 2 * TOK), 0)
    query_iota = lax.broadcasted_iota(jnp.int32, (TOK, 2 * TOK), 1)
    causal = key_iota <= query_iota % TOK

    for block in range(CTX):
        @pl.when(ctx != block)
        def _():
            for copy in inputs_to(zl, y, 0, block):
                copy.wait_recv()

        if block == 1:
            for copy in h_copies:
                copy.start()
        if block == 5:
            h_from_partner.wait_recv()
            for copy in h_passed:
                copy.start()

        first = max(0, block - SPAN)
        rows = slice(block * TOK, (block + 1) * TOK)
        band = slice(first * TOK, (block + 1) * TOK)
        deep = (block - first) * TOK
        seg_row = segs[block].astype(F32)
        segc[rows, :] = jnp.transpose(jnp.broadcast_to(seg_row, (TOK, TOK)))
        seg_row = jnp.concatenate([seg_row, seg_row], axis=1)
        seg_col = segc[band, :]
        seg_col = jnp.concatenate([seg_col, seg_col], axis=1)
        q2 = jnp.concatenate([qs[rows, :HD], qs[rows, HD:]], axis=0)
        do2 = jnp.concatenate([dos[rows, :HD], dos[rows, HD:]], axis=0)
        kw = ks[band, :]
        same = seg_col == seg_row
        scores = dot(kw, q2, NT)
        last = jnp.where(same[deep:] & causal, scores[deep:], FLOOR)
        if deep:
            scores = jnp.concatenate([jnp.where(same[:deep], scores[:deep], FLOOR), last], axis=0)
        else:
            scores = last
        peak = jnp.max(scores, axis=0, keepdims=True)
        weights = jnp.exp2((scores - peak) * EXP2_SCALE)
        probs = weights * (1.0 / jnp.sum(weights, axis=0, keepdims=True))
        probs_b = probs.astype(BF16)
        dprobs = dot(vs[band, :], do2, NT)
        delta = jnp.sum(probs_b.astype(F32) * dprobs, axis=0, keepdims=True)
        dscores = (probs * (dprobs - delta)).astype(BF16)
        dq2 = (dot(dscores, kw, TN) * SCALE).astype(BF16)
        dqs[rows, :HD] = dq2[:TOK]
        dqs[rows, HD:] = dq2[TOK:]
        start_out(0, block)
        dk_add = dot(dscores, q2)
        dv_add = dot(probs_b, do2)
        dka[rows, :] = dk_add[deep:]
        dva[rows, :] = dv_add[deep:]
        if deep:
            before = slice(first * TOK, block * TOK)
            dka[before, :] += dk_add[:deep]
            dva[before, :] += dv_add[:deep]
        if block >= SPAN:
            finish_keys(block - SPAN)
    for block in range(CTX - SPAN, CTX):
        finish_keys(block)

    h_own.wait()
    for dl in range(2):
        for dy in range(1, NY):
            sender = ((zl + dl) % 2) * NY + (y + dy) % NY
            remote(
                hs.at[zl], hall.at[:, at(sender, TOK)], hsend.at[0], hrecv.at[sender], (dp, partner)
            ).wait_recv()
    for block in range(CTX):
        for copy in trade(block, False):
            copy.wait_recv()

    def columns(kind):
        return jnp.concatenate([g4[2 * kind], g4[2 * kind + 1]], axis=1)

    far_core = (core + 1) % NC

    def core_copy(block):
        return remote(
            csend.at[block], crecv.at[block], csem.at[block], crsem.at[block],
            place(x, zh, far_core, zl, y),
        )

    for step in range(1, NX + 1):
        block = (x + step) % NX
        csend[block] = dot(hall[at(block, xrows), :], columns(far_core)).astype(BF16)
        core_copy(block).start()

    def x_copy(step, block):
        return remote(
            xsend.at[step], xrecv.at[step], xsem.at[step], xrsem.at[step],
            place(block, zh, core, zl, y),
        )

    for step in range(1, NX + 1):
        block = (x + step) % NX
        wown[...] = dot(hall[at(block, xrows), :], columns(core))
        core_copy(block).wait_recv()
        if step < NX:
            xsend[step - 1] = (wown[...] + crecv[block].astype(F32)).astype(BF16)
            x_copy(step - 1, block).start()
        else:
            tsum[:xrows, :] = wown[...] + crecv[block].astype(F32)
    for step in range(NX - 1):
        x_copy(step, x).wait_recv()
    tsum[:xrows, :] += (
        xrecv[0].astype(F32) + xrecv[1].astype(F32) + xrecv[2].astype(F32)
    )
    tsum[xrows:, :] = jnp.zeros((tsum.shape[0] - xrows, tsum.shape[1]), F32)

    def z_copies(piece):
        nz = 2 * zl + piece // 2
        nc = piece % 2
        mine = (nz == zh) & (nc == core) & (core == zl)
        return (
            mine,
            remote(
                zsend.at[piece], zrecv.at[zh], zsem.at[piece], zrsem.at[zh],
                place(x, nz, nc, core, y),
            ),
            pltpu.make_async_copy(zsend.at[piece], zrecv.at[zh], zsem.at[piece]),
        )

    for piece in range(4):
        zsend[piece] = tsum[piece * frows : piece * frows + zrows, :].astype(BF16)
        mine, far, near = z_copies(piece)

        @pl.when(mine)
        def _():
            near.start()

        @pl.when(jnp.logical_not(mine))
        def _():
            far.start()

    for piece in range(4):
        mine, far, near = z_copies(piece)

        @pl.when(mine)
        def _():
            near.wait()

        @pl.when(jnp.logical_not(mine))
        def _():
            far.wait_send()

    for sender in range(NZ):
        mine = (sender == zh) & (core == zl) & (zh // 2 == zl)

        @pl.when(jnp.logical_not(mine))
        def _():
            remote(
                zsend.at[0], zrecv.at[sender], zsem.at[0], zrsem.at[sender],
                place(x, zh, core, zl, y),
            ).wait_recv()

    w_out[...] = (
        (zrecv[0, :frows, :].astype(F32) + zrecv[1, :frows, :].astype(F32))
        + (zrecv[2, :frows, :].astype(F32) + zrecv[3, :frows, :].astype(F32))
    )

    for block in range(CTX):
        for index in range(3):
            far, near = out_sends(block)[index]

            @pl.when(ctx != block)
            def _():
                far.wait_send()

            @pl.when(ctx == block)
            def _():
                near.wait()

        for copy in trade(block, True):
            copy.wait_send()
    for block in range(CTX):
        from_head = 2 * (block % NY) + block // NY
        rows = pl.ds(0, TOK)

        @pl.when(ctx != block)
        def _():
            for index, (src, dst) in enumerate((
                (dqs.at[rows, :], dq_out.at[:, at(from_head, 2 * HD)]),
                (g4.at[0, rows, :], dk_out.at[:, at(from_head, HD)]),
                (g4.at[0, rows, :], dv_out.at[:, at(from_head, HD)]),
            )):
                remote(src, dst, osend.at[index, 0], orecv.at[index, block], (dp, partner)).wait_recv()

    for copy in input_copies + [h_across] + h_copies + h_passed:
        copy.wait_send()
    for step in range(1, NX + 1):
        core_copy((x + step) % NX).wait_send()
    for step in range(NX - 1):
        x_copy(step, x).wait_send()


def local(hidden_in, queries, key_states, value_states, out_grad, segment_ids):
    feats = hidden_in.shape[2]
    width = queries.shape[2]
    key_width = key_states.shape[2]
    half = feats // 2
    xrows = half // NX
    frows = feats // (NX * NZ * NC)
    zrows = -(-frows // 16) * 16
    seq = CTX * TOK
    any_spec = pl.BlockSpec(memory_space=pl.ANY)
    dma = pltpu.SemaphoreType.DMA
    scratch = [
        pltpu.VMEM((TOK, feats), BF16),
        pltpu.VMEM((seq, 2 * HD), BF16),
        pltpu.VMEM((seq, 2 * HD), BF16),
        pltpu.VMEM((seq, HD), BF16),
        pltpu.VMEM((seq, HD), BF16),
        pltpu.VMEM((CTX, 1, TOK), jnp.int32),
        pltpu.VMEM((seq, TOK), F32),
        pltpu.VMEM((seq, 2 * HD), BF16),
        pltpu.VMEM((4, seq, HD), BF16),
        pltpu.VMEM((seq, HD), F32),
        pltpu.VMEM((seq, HD), F32),
        pltpu.VMEM((2, half, TOK), BF16),
        pltpu.VMEM((half, seq), BF16),
        pltpu.VMEM((xrows, 2 * HD), F32),
        pltpu.VMEM((NX, xrows, 2 * HD), BF16),
        pltpu.VMEM((NX, xrows, 2 * HD), BF16),
        pltpu.VMEM((NX - 1, xrows, 2 * HD), BF16),
        pltpu.VMEM((NX - 1, xrows, 2 * HD), BF16),
        pltpu.VMEM((xrows + 16, 2 * HD), F32),
        pltpu.VMEM((4, zrows, 2 * HD), BF16),
        pltpu.VMEM((NZ, zrows, 2 * HD), BF16),
        dma((7,)),
        dma((5, 7)), dma((5, CTX)),
        dma((3, CTX)), dma((3, CTX)),
        dma((2, CTX)), dma((2, CTX)),
        dma((7,)), dma((CTX,)),
        dma((NX,)), dma((NX,)),
        dma((NX - 1,)), dma((NX - 1,)),
        dma((4,)), dma((NZ,)),
    ]
    dq, dk, dv, dw = pl.pallas_call(
        kernel,
        out_shape=(
            jax.ShapeDtypeStruct((TOK, width), BF16),
            jax.ShapeDtypeStruct((TOK, key_width), BF16),
            jax.ShapeDtypeStruct((TOK, key_width), BF16),
            jax.ShapeDtypeStruct((frows, 2 * HD), F32),
        ),
        in_specs=[any_spec] * 6,
        out_specs=(any_spec, any_spec, any_spec, pl.BlockSpec(memory_space=pltpu.VMEM)),
        scratch_shapes=scratch,
        compiler_params=pltpu.CompilerParams(
            collective_id=0, has_side_effects=True, vmem_limit_bytes=48 << 20
        ),
    )(hidden_in[0], queries[0], key_states[0], value_states[0], out_grad[0], segment_ids)
    return dq[None], dk[None], dv[None], dw


def solution(mesh):
    row = P("dp", "ctx", None)
    return jax.shard_map(
        local,
        mesh=mesh,
        in_specs=(row, row, row, row, row, P("dp", "ctx")),
        out_specs=(row, row, row, P("dp", "ctx")),
        check_vma=False,
    )
```

time: 631 us -> 100 us (0.16)
  waiting for transfers between devices: 368 us -> 0 us
  matrix products: 102 us -> 0 us
  Pallas kernels: 0 us -> 90.7 us
  starting transfers between devices: 81.3 us -> 0 us
  local copies, waits for them, and re-layouts: 36.5 us -> 8.57 us
  between operations: 15.4 us -> 0.66 us
  other arithmetic: 13.5 us -> 0 us
  blocking collectives: 10 us -> 0 us
    unnamed x3 -> x0, waiting for transfers between devices: 287 us -> none
    pallas_call x0 -> x1, Pallas kernels: none -> 90.7 us  [local(): pl.pallas_call(kernel, out_shape=(jax.ShapeDtypeStruct((TOK, width), BF16...]
    ppermute x35 -> x0, starting transfers between devices: 81.2 us -> none  [shifted(): lax.ppermute(value, axis, [(source, source + steps) for source in range(l...]
    ppermute x35 -> x0, waiting for transfers between devices: 81 us -> none  [shifted(): lax.ppermute(value, axis, [(source, source + steps) for source in range(l...]
    dot_general x41 -> x0, matrix products: 80.9 us -> none  [the longest x8 20.4 us: head_grads(): jnp.einsum('gij,igd->jd', probs_low, grad_head, preferred_element_type=jn...]
    sub x8 -> x0, matrix products: 20.8 us -> none  [head_grads(): weights = jnp.where(allowed[None], jnp.exp(scores - row_peak), 0.0)]
    slice x14 -> x0, local copies, waits for them, and re-layouts: 16.4 us -> none  [the longest x7 9.8 us: local(): value_rows[lower_row:lower_row + tok_rows]]
    all_to_all x1 -> x0, blocking collectives: 10 us -> none  [local(): lax.all_to_all(both_grads, 'ctx', split_axis=1, concat_axis=0, tiled=True)]
  transfers between devices with their start and end apart: 37 -> 0, of which waited for: 15 -> 0; matrix products, arithmetic and copies ran while one was open for 23% -> 0% of each run, Pallas kernels for 0% -> 0%
where the time goes in v1:
time: 100 us; the launch traced here: 99.9 us
  Pallas kernels  90.7 us (91%)
  local copies, waits for them, and re-layouts  8.57 us (9%)
    pallas_call x1, Pallas kernels, local(): pl.pallas_call(kernel, out_shape=(jax.ShapeDtypeStruct((TOK, width), BF16...  90.7 us
    unnamed x16, local copies, waits for them, and re-layouts  8.57 us

profile of v1, /device:TPU:1, one launch (start us, length us, event | category | flops | bytes accessed | tf_op | source)
XLA Modules:
  0.0 99.9 jit_solution(2155071914024676360)
XLA Ops:
  0.6 0.0 copy-start.5
  0.6 0.6 copy-done.5
  1.3 0.0 copy-start
  1.3 1.1 %copy-done = bf16[1,128,2688]{2,1,0:T(8,128)(2,1)S(1)} copy-done((bf16[1,128,2688]{2,1,0:T(8,128)(2,1)S(1)}, bf16[1,128,2688]{2,1,0:T(8,128)(2,1)}, u32[]{:S(2)}) %copy-start) | copy-done | bytes 688152
  2.4 0.0 copy-start.1
  2.4 1.0 %copy-done.1 = bf16[1,128,2048]{2,1,0:T(8,128)(2,1)S(1)} copy-done((bf16[1,128,2048]{2,1,0:T(8,128)(2,1)S(1)}, bf16[1,128,2048]{2,1,0:T(8,128)(2,1)}, u32[]{:S(2)}) %copy-start.1) | copy-done | bytes 524312
  3.4 0.0 copy-start.2
  3.4 1.0 %copy-done.2 = bf16[1,128,2048]{2,1,0:T(8,128)(2,1)S(1)} copy-done((bf16[1,128,2048]{2,1,0:T(8,128)(2,1)S(1)}, bf16[1,128,2048]{2,1,0:T(8,128)(2,1)}, u32[]{:S(2)}) %copy-start.2) | copy-done | bytes 524312
  4.5 0.0 copy-start.3
  4.5 0.9 copy-done.3
  5.4 0.0 copy-start.4
  5.4 0.9 copy-done.4
  6.4 90.7 %shard_map.93 = (bf16[128,2048]{1,0:T(8,128)(2,1)S(1)}, bf16[128,1024]{1,0:T(8,128)(2,1)S(1)}, bf16[128,1024]{1,0:T(8,128)(2,1)S(1)}, f32[84,256]{1,0:T(8,128)S(1)}) custom-call(bf16[128,2688]{1,0:T(8,128)(2,1)S(1)} %bitcast.8, bf16[128,2048]{1,0:T(8,128)(2,1)S(1)} %bitcast.9, bf16[128,1024]{1,0:T(8,128)(2,1)S(1)} %bitcast.12, ...), custom_call_target="tpu_custom_call" | custom-call | tf_op jit(solution)/shard_map/pallas_call | solution.py:452
  97.0 0.8 copy.14
  97.8 0.7 copy.15
  98.5 0.7 copy.16
  99.2 0.6 copy.17
Async XLA Ops:
  0.6 0.7 copy-start.5
  1.3 1.1 %copy-start = (bf16[1,128,2688]{2,1,0:T(8,128)(2,1)S(1)}, bf16[1,128,2688]{2,1,0:T(8,128)(2,1)}, u32[]{:S(2)}) copy-start(bf16[1,128,2688]{2,1,0:T(8,128)(2,1)} %param.6) | copy-start | bytes 2064388
  2.4 1.0 %copy-start.1 = (bf16[1,128,2048]{2,1,0:T(8,128)(2,1)S(1)}, bf16[1,128,2048]{2,1,0:T(8,128)(2,1)}, u32[]{:S(2)}) copy-start(bf16[1,128,2048]{2,1,0:T(8,128)(2,1)} %param.7) | copy-start | bytes 1572868
  3.4 1.0 %copy-start.2 = (bf16[1,128,2048]{2,1,0:T(8,128)(2,1)S(1)}, bf16[1,128,2048]{2,1,0:T(8,128)(2,1)}, u32[]{:S(2)}) copy-start(bf16[1,128,2048]{2,1,0:T(8,128)(2,1)} %param.10) | copy-start | bytes 1572868
  4.5 0.9 copy-start.3
  5.4 0.9 copy-start.4

commit v2 on v1

--- a/solution.py
+++ b/solution.py
@@ -34,7 +34,8 @@
     h, q, k, v, do, seg, dq_out, dk_out, dv_out, w_out,
     hv, qs, dos, ks, vs, segs, segc, dqs, g4, dka, dva, hs, hall,
     wown, csend, crecv, xsend, xrecv, tsum, zsend, zrecv,
-    lsem, asend, arecv, osend, orecv, gsend, grecv, hsend, hrecv,
+    lsem, asend, arecv, osend, orecv, gsend, grecv,
+    hasend, harecv, hysend, hyrecv, hpsend, hprecv,
     csem, crsem, xsem, xrsem, zsem, zrsem,
 ):
     feats = h.shape[1]
@@ -42,6 +43,7 @@
     xrows = half // NX
     frows = w_out.shape[0]
     zrows = zsend.shape[1]
+    split = (xrows // 2 + 15) // 16 * 16
     dp = lax.axis_index("dp")
     ctx = lax.axis_index("ctx")
     x = dp // (NZ * NC)
@@ -138,58 +140,95 @@
             ]
             row = stop
 
-    h_across = remote(
-        hs.at[other], hall.at[:, own], hsend.at[0], hrecv.at[ctx], (dp, partner)
-    )
-    h_across.start()
     h_own = pltpu.make_async_copy(hs.at[zl], hall.at[:, own], lsem.at[6])
     h_own.start()
-    h_copies = [
-        remote(
-            hs.at[zl], hall.at[:, own], hsend.at[dy], hrecv.at[ctx],
-            (dp, zl * NY + (y + dy) % NY),
-        )
-        for dy in (2, 1, 3)
-    ]
-    theirs = at(partner, TOK)
-    h_passed = [
-        remote(
-            hall.at[:, theirs], hall.at[:, theirs], hsend.at[NY - 1 + dy], hrecv.at[partner],
-            (dp, zl * NY + (y + dy) % NY),
-        )
-        for dy in (2, 1, 3)
-    ]
-    h_from_partner = remote(
-        hs.at[other], hall.at[:, theirs], hsend.at[0], hrecv.at[partner], (dp, partner)
-    )
+
+    def chunk(step):
+        return (x + step + 1) % NX * xrows
+
+    def h_rows(step, part=None):
+        start, size = (0, xrows) if part is None else ((0, split), (split, xrows - split))[part]
+        return pl.ds(pl.multiple_of(chunk(step) + start, 16), size)
+
+    def h_across(step, block):
+        return remote(
+            hs.at[other, h_rows(step), :], hall.at[h_rows(step), at(block, TOK)],
+            hasend.at[step], harecv.at[step], (dp, partner),
+        )
+
+    def h_block(kind, ny):
+        return (zl + kind) % 2 * NY + (ny + NY) % NY
+
+    def h_step(step, kind, way, ny):
+        cols = at(h_block(kind, ny), TOK)
+        src = hall.at[h_rows(step), cols] if kind else hs.at[zl, h_rows(step), :]
+        return remote(
+            src, hall.at[h_rows(step), cols], hysend.at[step, kind, way],
+            hyrecv.at[step, kind, way], (dp, zl * NY + (y + 1 + 2 * way) % NY),
+        )
+
+    def h_pass(step, kind, way, ny):
+        place_of = hall.at[h_rows(step, way), at(h_block(kind, ny), TOK)]
+        return remote(
+            place_of, place_of, hpsend.at[step, kind, way],
+            hprecv.at[step, kind, way], (dp, zl * NY + (y + 1 + 2 * way) % NY),
+        )
+
+    def h_start(step, kind):
+        for way in range(2):
+            h_step(step, kind, way, y).start()
+
+    def h_forward(step, kind):
+        for way in range(2):
+            came_from = y - 1 + 2 * way
+            h_step(step, kind, way, came_from).wait_recv()
+            h_pass(step, kind, way, came_from).start()
+
+    def h_arrive(step):
+        for kind in range(2):
+            for way in range(2):
+                h_pass(step, kind, way, y + 2).wait_recv()
+
+    def h_partner(step):
+        h_across(step, partner).wait_recv()
+        h_start(step, 1)
+
+    h_across(0, ctx).start()
+    h_across(1, ctx).start()
+    h_across(2, ctx).start()
+    h_across(3, ctx).start()
+    h_start(0, 0)
+    h_start(1, 0)
+    h_start(2, 0)
+    h_start(3, 0)
 
     for copy in local_in[1:]:
         copy.wait()
 
-    def out_copy(index, src, dst, block):
-        return (
-            remote(src, dst, osend.at[index, block], orecv.at[index, ctx], (dp, block)),
-            pltpu.make_async_copy(src, dst, osend.at[index, block]),
-        )
-
-    def out_sends(block):
+    def out_refs(index, block):
         rows = pl.ds(block * TOK, TOK)
         return (
-            out_copy(0, dqs.at[rows, :], dq_out.at[:, at(head, 2 * HD)], block),
-            out_copy(1, g4.at[zl, rows, :], dk_out.at[:, at(head, HD)], block),
-            out_copy(2, g4.at[2 + zl, rows, :], dv_out.at[:, at(head, HD)], block),
-        )
+            (dqs.at[rows, :], dq_out.at[:, at(head, 2 * HD)]),
+            (g4.at[zl, rows, :], dk_out.at[:, at(head, HD)]),
+            (g4.at[2 + zl, rows, :], dv_out.at[:, at(head, HD)]),
+        )[index]
+
+    def out_far(index, block):
+        return remote(
+            *out_refs(index, block), osend.at[index, block], orecv.at[index, ctx], (dp, block)
+        )
+
+    def out_near(index, block):
+        return pltpu.make_async_copy(*out_refs(index, block), osend.at[index, block])
 
     def start_out(index, block):
-        far, near = out_sends(block)[index]
-
         @pl.when(ctx != block)
         def _():
-            far.start()
+            out_far(index, block).start()
 
         @pl.when(ctx == block)
         def _():
-            near.start()
+            out_near(index, block).start()
 
     def trade(block, mine):
         rows = pl.ds(block * TOK, TOK)
@@ -208,8 +247,6 @@
         g4[2 + zl, rows, :] = dva[rows, :].astype(BF16)
         for copy in trade(block, True):
             copy.start()
-        start_out(1, block)
-        start_out(2, block)
 
     key_iota = lax.broadcasted_iota(jnp.int32, (TOK, 2 * TOK), 0)
     query_iota = lax.broadcasted_iota(jnp.int32, (TOK, 2 * TOK), 1)
@@ -221,13 +258,15 @@
             for copy in inputs_to(zl, y, 0, block):
                 copy.wait_recv()
 
-        if block == 1:
-            for copy in h_copies:
-                copy.start()
         if block == 5:
-            h_from_partner.wait_recv()
-            for copy in h_passed:
-                copy.start()
+            h_forward(0, 0)
+            h_forward(1, 0)
+        if block == 6:
+            h_partner(0)
+            h_partner(1)
+        if block == 7:
+            h_partner(2)
+            h_partner(3)
 
         first = max(0, block - SPAN)
         rows = slice(block * TOK, (block + 1) * TOK)
@@ -258,7 +297,6 @@
         dq2 = (dot(dscores, kw, TN) * SCALE).astype(BF16)
         dqs[rows, :HD] = dq2[:TOK]
         dqs[rows, HD:] = dq2[TOK:]
-        start_out(0, block)
         dk_add = dot(dscores, q2)
         dv_add = dot(probs_b, do2)
         dka[rows, :] = dk_add[deep:]
@@ -272,17 +310,6 @@
     for block in range(CTX - SPAN, CTX):
         finish_keys(block)
 
-    h_own.wait()
-    for dl in range(2):
-        for dy in range(1, NY):
-            sender = ((zl + dl) % 2) * NY + (y + dy) % NY
-            remote(
-                hs.at[zl], hall.at[:, at(sender, TOK)], hsend.at[0], hrecv.at[sender], (dp, partner)
-            ).wait_recv()
-    for block in range(CTX):
-        for copy in trade(block, False):
-            copy.wait_recv()
-
     def columns(kind):
         return jnp.concatenate([g4[2 * kind], g4[2 * kind + 1]], axis=1)
 
@@ -294,26 +321,54 @@
             place(x, zh, far_core, zl, y),
         )
 
-    for step in range(1, NX + 1):
-        block = (x + step) % NX
+    def x_copy(step, block):
+        return remote(
+            xsend.at[step], xrecv.at[step], xsem.at[step], xrsem.at[step],
+            place(block, zh, core, zl, y),
+        )
+
+    def weights_far(step):
+        block = (x + step + 1) % NX
+        h_arrive(step)
+        if step == 0:
+            h_own.wait()
+            for block_in in range(CTX):
+                for copy in trade(block_in, False):
+                    copy.wait_recv()
         csend[block] = dot(hall[at(block, xrows), :], columns(far_core)).astype(BF16)
         core_copy(block).start()
 
-    def x_copy(step, block):
-        return remote(
-            xsend.at[step], xrecv.at[step], xsem.at[step], xrsem.at[step],
-            place(block, zh, core, zl, y),
-        )
-
-    for step in range(1, NX + 1):
-        block = (x + step) % NX
+    def weights_own(step):
+        block = (x + step + 1) % NX
         wown[...] = dot(hall[at(block, xrows), :], columns(core))
         core_copy(block).wait_recv()
-        if step < NX:
-            xsend[step - 1] = (wown[...] + crecv[block].astype(F32)).astype(BF16)
-            x_copy(step - 1, block).start()
+        if step < NX - 1:
+            xsend[step] = (wown[...] + crecv[block].astype(F32)).astype(BF16)
+            x_copy(step, block).start()
         else:
             tsum[:xrows, :] = wown[...] + crecv[block].astype(F32)
+
+    def give_back():
+        for block in range(CTX):
+            for index in range(3):
+                start_out(index, block)
+
+    h_forward(2, 0)
+    h_forward(3, 0)
+    h_forward(0, 1)
+    h_forward(1, 1)
+    h_forward(2, 1)
+    weights_far(0)
+    h_forward(3, 1)
+    weights_far(1)
+    weights_own(0)
+    give_back()
+    weights_far(2)
+    weights_own(1)
+    weights_far(3)
+    weights_own(2)
+    weights_own(3)
+
     for step in range(NX - 1):
         x_copy(step, x).wait_recv()
     tsum[:xrows, :] += (
@@ -321,41 +376,37 @@
     )
     tsum[xrows:, :] = jnp.zeros((tsum.shape[0] - xrows, tsum.shape[1]), F32)
 
-    def z_copies(piece):
-        nz = 2 * zl + piece // 2
-        nc = piece % 2
-        mine = (nz == zh) & (nc == core) & (core == zl)
-        return (
-            mine,
-            remote(
-                zsend.at[piece], zrecv.at[zh], zsem.at[piece], zrsem.at[zh],
-                place(x, nz, nc, core, y),
-            ),
-            pltpu.make_async_copy(zsend.at[piece], zrecv.at[zh], zsem.at[piece]),
-        )
+    def z_mine(piece):
+        return (2 * zl + piece // 2 == zh) & (piece % 2 == core) & (core == zl)
+
+    def z_far(piece):
+        return remote(
+            zsend.at[piece], zrecv.at[zh], zsem.at[piece], zrsem.at[zh],
+            place(x, 2 * zl + piece // 2, piece % 2, core, y),
+        )
+
+    def z_near(piece):
+        return pltpu.make_async_copy(zsend.at[piece], zrecv.at[zh], zsem.at[piece])
 
     for piece in range(4):
         zsend[piece] = tsum[piece * frows : piece * frows + zrows, :].astype(BF16)
-        mine, far, near = z_copies(piece)
-
-        @pl.when(mine)
-        def _():
-            near.start()
-
-        @pl.when(jnp.logical_not(mine))
-        def _():
-            far.start()
+
+        @pl.when(z_mine(piece))
+        def _():
+            z_near(piece).start()
+
+        @pl.when(jnp.logical_not(z_mine(piece)))
+        def _():
+            z_far(piece).start()
 
     for piece in range(4):
-        mine, far, near = z_copies(piece)
-
-        @pl.when(mine)
-        def _():
-            near.wait()
-
-        @pl.when(jnp.logical_not(mine))
-        def _():
-            far.wait_send()
+        @pl.when(z_mine(piece))
+        def _():
+            z_near(piece).wait()
+
+        @pl.when(jnp.logical_not(z_mine(piece)))
+        def _():
+            z_far(piece).wait_send()
 
     for sender in range(NZ):
         mine = (sender == zh) & (core == zl) & (zh // 2 == zl)
@@ -374,15 +425,13 @@
 
     for block in range(CTX):
         for index in range(3):
-            far, near = out_sends(block)[index]
-
             @pl.when(ctx != block)
             def _():
-                far.wait_send()
+                out_far(index, block).wait_send()
 
             @pl.when(ctx == block)
             def _():
-                near.wait()
+                out_near(index, block).wait()
 
         for copy in trade(block, True):
             copy.wait_send()
@@ -399,12 +448,38 @@
             )):
                 remote(src, dst, osend.at[index, 0], orecv.at[index, block], (dp, partner)).wait_recv()
 
-    for copy in input_copies + [h_across] + h_copies + h_passed:
+    for copy in input_copies:
         copy.wait_send()
+    for step in range(NX):
+        h_across(step, ctx).wait_send()
+        for kind in range(2):
+            for way in range(2):
+                h_step(step, kind, way, y).wait_send()
+                h_pass(step, kind, way, y - 1 + 2 * way).wait_send()
     for step in range(1, NX + 1):
         core_copy((x + step) % NX).wait_send()
     for step in range(NX - 1):
         x_copy(step, x).wait_send()
+
+
+def hand_over(*refs):
+    sources, targets, stages = refs[:4], refs[4:8], refs[8:12]
+    sems = refs[12]
+    loads = [
+        pltpu.make_async_copy(src, stage, sems.at[0, index])
+        for index, (src, stage) in enumerate(zip(sources, stages))
+    ]
+    stores = [
+        pltpu.make_async_copy(stage, dst, sems.at[1, index])
+        for index, (stage, dst) in enumerate(zip(stages, targets))
+    ]
+    for copy in loads:
+        copy.start()
+    for load, store in zip(loads, stores):
+        load.wait()
+        store.start()
+    for copy in stores:
+        copy.wait()
 
 
 def local(hidden_in, queries, key_states, value_states, out_grad, segment_ids):
@@ -416,7 +491,7 @@
     frows = feats // (NX * NZ * NC)
     zrows = -(-frows // 16) * 16
     seq = CTX * TOK
-    any_spec = pl.BlockSpec(memory_space=pl.ANY)
+    any_spec = pl.BlockSpec(memory_space=pltpu.HBM)
     dma = pltpu.SemaphoreType.DMA
     scratch = [
         pltpu.VMEM((TOK, feats), BF16),
@@ -444,26 +519,36 @@
         dma((5, 7)), dma((5, CTX)),
         dma((3, CTX)), dma((3, CTX)),
         dma((2, CTX)), dma((2, CTX)),
-        dma((7,)), dma((CTX,)),
+        dma((NX,)), dma((NX,)),
+        dma((NX, 2, 2)), dma((NX, 2, 2)),
+        dma((NX, 2, 2)), dma((NX, 2, 2)),
         dma((NX,)), dma((NX,)),
         dma((NX - 1,)), dma((NX - 1,)),
         dma((4,)), dma((NZ,)),
     ]
-    dq, dk, dv, dw = pl.pallas_call(
+    outs = (
+        jax.ShapeDtypeStruct((TOK, width), BF16),
+        jax.ShapeDtypeStruct((TOK, key_width), BF16),
+        jax.ShapeDtypeStruct((TOK, key_width), BF16),
+        jax.ShapeDtypeStruct((frows, 2 * HD), F32),
+    )
+    parts = pl.pallas_call(
         kernel,
-        out_shape=(
-            jax.ShapeDtypeStruct((TOK, width), BF16),
-            jax.ShapeDtypeStruct((TOK, key_width), BF16),
-            jax.ShapeDtypeStruct((TOK, key_width), BF16),
-            jax.ShapeDtypeStruct((frows, 2 * HD), F32),
-        ),
+        out_shape=outs,
         in_specs=[any_spec] * 6,
         out_specs=(any_spec, any_spec, any_spec, pl.BlockSpec(memory_space=pltpu.VMEM)),
         scratch_shapes=scratch,
         compiler_params=pltpu.CompilerParams(
-            collective_id=0, has_side_effects=True, vmem_limit_bytes=48 << 20
+            collective_id=0, has_side_effects=True, vmem_limit_bytes=63 << 20
         ),
     )(hidden_in[0], queries[0], key_states[0], value_states[0], out_grad[0], segment_ids)
+    dq, dk, dv, dw = pl.pallas_call(
+        hand_over,
+        out_shape=outs,
+        in_specs=[any_spec] * 4,
+        out_specs=(any_spec,) * 4,
+        scratch_shapes=[pltpu.VMEM(out.shape, out.dtype) for out in outs] + [dma((2, 4))],
+    )(*parts)
     return dq[None], dk[None], dv[None], dw
 
 

time: 100 us -> 75.5 us (0.76)
  Pallas kernels: 90.7 us -> 74.8 us
  local copies, waits for them, and re-layouts: 8.57 us -> 0 us
    pallas_call x1 -> x2, Pallas kernels: 90.7 us -> 74.8 us  [the longest x1 72.7 us: local(): pl.pallas_call(kernel, out_shape=outs, in_specs=[any_spec] * 6, out_specs...]
    unnamed x16 -> x0, local copies, waits for them, and re-layouts: 8.57 us -> none
where the time goes in v2:
time: 75.5 us; the launch traced here: 75.4 us
  Pallas kernels  74.8 us (99%)
    pallas_call x1, Pallas kernels, local(): pl.pallas_call(kernel, out_shape=outs, in_specs=[any_spec] * 6, out_specs...  72.7 us
    pallas_call x1, Pallas kernels, local(): pl.pallas_call(hand_over, out_shape=outs, in_specs=[any_spec] * 4, out_sp...  2.09 us

profile of v2, /device:TPU:1, one launch (start us, length us, event | category | flops | bytes accessed | tf_op | source)
XLA Modules:
  0.0 75.4 jit_solution(16649402751853409193)
XLA Ops:
  0.6 72.7 %shard_map.93 = (bf16[128,2048]{1,0:T(8,128)(2,1)}, bf16[128,1024]{1,0:T(8,128)(2,1)}, bf16[128,1024]{1,0:T(8,128)(2,1)}, f32[84,256]{1,0:T(8,128)}) custom-call(bf16[128,2688]{1,0:T(8,128)(2,1)} %bitcast.8, bf16[128,2048]{1,0:T(8,128)(2,1)} %bitcast.9, bf16[128,1024]{1,0:T(8,128)(2,1)} %bitcast.11, bf16[128,1024]{1,0:T(8,128)(2,1)} %bitcast.12, ...), custom_call_target="tpu_custom_call" | custom-call | tf_op jit(solution)/shard_map/pallas_call | solution.py:535
  73.3 2.1 %shard_map.94 = (bf16[128,2048]{1,0:T(8,128)(2,1)}, bf16[128,1024]{1,0:T(8,128)(2,1)}, bf16[128,1024]{1,0:T(8,128)(2,1)}, f32[84,256]{1,0:T(8,128)}) custom-call(bf16[128,2048]{1,0:T(8,128)(2,1)} %get-tuple-element.12.refs_0_, bf16[128,1024]{1,0:T(8,128)(2,1)} %get-tuple-element.13.refs_1_, bf16[128,1024]{1,0:T(8,128)(2,1)} %get-tuple-element.14.refs_2_, ...), custom_call_target="tpu_custom_call" | custom-call | tf_op jit(solution)/shard_map/pallas_call | solution.py:545

commit v3 on v2

--- a/solution.py
+++ b/solution.py
@@ -22,6 +22,7 @@
 F32 = jnp.float32
 BF16 = jnp.bfloat16
 PEERS = ((1, 2), (0, 2), (1, 1), (1, 3), (0, 1), (0, 3), (1, 0))
+ORDER = (1, 2, 3, 0)
 NT = (((1,), (1,)), ((), ()))
 TN = (((0,), (0,)), ((), ()))
 
@@ -33,9 +34,9 @@
 def kernel(
     h, q, k, v, do, seg, dq_out, dk_out, dv_out, w_out,
     hv, qs, dos, ks, vs, segs, segc, dqs, g4, dka, dva, hs, hall,
-    wown, csend, crecv, xsend, xrecv, tsum, zsend, zrecv,
+    csend, crecv, xsend, xrecv, tsum, zsend, zrecv,
     lsem, asend, arecv, osend, orecv, gsend, grecv,
-    hasend, harecv, hysend, hyrecv, hpsend, hprecv,
+    hsend, harecv, hyrecv, hprecv,
     csem, crsem, xsem, xrsem, zsem, zrsem,
 ):
     feats = h.shape[1]
@@ -66,6 +67,10 @@
             src_ref=src, dst_ref=dst, send_sem=ssem, recv_sem=rsem,
             device_id=device, device_id_type=MESH,
         )
+
+    def drain(sem, rows, cols):
+        whole = hall.at[pl.ds(0, rows), pl.ds(0, cols)]
+        pltpu.make_async_copy(whole, whole, sem).wait()
 
     barrier = pltpu.get_barrier_semaphore()
     count = 0
@@ -105,7 +110,7 @@
         copy.start()
     pl.semaphore_wait(barrier, count)
 
-    def inputs_to(nl, ny, slot, sender):
+    def inputs_to(nl, ny, sender, slot=0):
         to_head = 2 * ny + nl
         target = (dp, nl * NY + ny)
         rows = at(sender, TOK)
@@ -117,13 +122,13 @@
             (seg, segs.at[sender]),
         )
         return [
-            remote(src, dst, asend.at[index, slot], arecv.at[index, sender], target)
+            remote(src, dst, asend.at[index // 4 * (1 + slot)], arecv.at[index // 4, sender], target)
             for index, (src, dst) in enumerate(pairs)
         ]
 
     input_copies = []
     for slot, (dl, dy) in enumerate(PEERS):
-        input_copies += inputs_to((zl + dl) % 2, (y + dy) % NY, slot, ctx)
+        input_copies += inputs_to((zl + dl) % 2, (y + dy) % NY, ctx, slot)
     for copy in input_copies:
         copy.start()
 
@@ -143,8 +148,11 @@
     h_own = pltpu.make_async_copy(hs.at[zl], hall.at[:, own], lsem.at[6])
     h_own.start()
 
+    def x_of(step):
+        return (x + ORDER[step]) % NX
+
     def chunk(step):
-        return (x + step + 1) % NX * xrows
+        return x_of(step) * xrows
 
     def h_rows(step, part=None):
         start, size = (0, xrows) if part is None else ((0, split), (split, xrows - split))[part]
@@ -153,7 +161,7 @@
     def h_across(step, block):
         return remote(
             hs.at[other, h_rows(step), :], hall.at[h_rows(step), at(block, TOK)],
-            hasend.at[step], harecv.at[step], (dp, partner),
+            hsend.at[0], harecv.at[step], (dp, partner),
         )
 
     def h_block(kind, ny):
@@ -163,15 +171,15 @@
         cols = at(h_block(kind, ny), TOK)
         src = hall.at[h_rows(step), cols] if kind else hs.at[zl, h_rows(step), :]
         return remote(
-            src, hall.at[h_rows(step), cols], hysend.at[step, kind, way],
-            hyrecv.at[step, kind, way], (dp, zl * NY + (y + 1 + 2 * way) % NY),
+            src, hall.at[h_rows(step), cols], hsend.at[0],
+            hyrecv.at[step, kind], (dp, zl * NY + (y + 1 + 2 * way) % NY),
         )
 
     def h_pass(step, kind, way, ny):
         place_of = hall.at[h_rows(step, way), at(h_block(kind, ny), TOK)]
         return remote(
-            place_of, place_of, hpsend.at[step, kind, way],
-            hprecv.at[step, kind, way], (dp, zl * NY + (y + 1 + 2 * way) % NY),
+            place_of, place_of, hsend.at[0],
+            hprecv.at[step], (dp, zl * NY + (y + 1 + 2 * way) % NY),
         )
 
     def h_start(step, kind):
@@ -179,15 +187,12 @@
             h_step(step, kind, way, y).start()
 
     def h_forward(step, kind):
+        drain(hyrecv.at[step, kind], xrows, 2 * TOK)
         for way in range(2):
-            came_from = y - 1 + 2 * way
-            h_step(step, kind, way, came_from).wait_recv()
-            h_pass(step, kind, way, came_from).start()
+            h_pass(step, kind, way, y - 1 + 2 * way).start()
 
     def h_arrive(step):
-        for kind in range(2):
-            for way in range(2):
-                h_pass(step, kind, way, y + 2).wait_recv()
+        drain(hprecv.at[step], xrows, 2 * TOK)
 
     def h_partner(step):
         h_across(step, partner).wait_recv()
@@ -195,48 +200,26 @@
 
     h_across(0, ctx).start()
     h_across(1, ctx).start()
-    h_across(2, ctx).start()
-    h_across(3, ctx).start()
     h_start(0, 0)
     h_start(1, 0)
-    h_start(2, 0)
-    h_start(3, 0)
 
     for copy in local_in[1:]:
         copy.wait()
 
-    def out_refs(index, block):
-        rows = pl.ds(block * TOK, TOK)
+    def out_refs(block):
+        rows = at(block, TOK)
         return (
             (dqs.at[rows, :], dq_out.at[:, at(head, 2 * HD)]),
             (g4.at[zl, rows, :], dk_out.at[:, at(head, HD)]),
             (g4.at[2 + zl, rows, :], dv_out.at[:, at(head, HD)]),
-        )[index]
-
-    def out_far(index, block):
-        return remote(
-            *out_refs(index, block), osend.at[index, block], orecv.at[index, ctx], (dp, block)
-        )
-
-    def out_near(index, block):
-        return pltpu.make_async_copy(*out_refs(index, block), osend.at[index, block])
-
-    def start_out(index, block):
-        @pl.when(ctx != block)
-        def _():
-            out_far(index, block).start()
-
-        @pl.when(ctx == block)
-        def _():
-            out_near(index, block).start()
-
-    def trade(block, mine):
+        )
+
+    def trade(block):
         rows = pl.ds(block * TOK, TOK)
-        which = zl if mine else other
         return [
             remote(
-                g4.at[2 * kind + which, rows, :], g4.at[2 * kind + which, rows, :],
-                gsend.at[kind, block], grecv.at[kind, block], (dp, partner),
+                g4.at[2 * kind + zl, rows, :], g4.at[2 * kind + zl, rows, :],
+                gsend.at[0], grecv.at[0], (dp, partner),
             )
             for kind in range(2)
         ]
@@ -245,7 +228,7 @@
         rows = slice(block * TOK, (block + 1) * TOK)
         g4[zl, rows, :] = (dka[rows, :] * SCALE).astype(BF16)
         g4[2 + zl, rows, :] = dva[rows, :].astype(BF16)
-        for copy in trade(block, True):
+        for copy in trade(block):
             copy.start()
 
     key_iota = lax.broadcasted_iota(jnp.int32, (TOK, 2 * TOK), 0)
@@ -255,9 +238,14 @@
     for block in range(CTX):
         @pl.when(ctx != block)
         def _():
-            for copy in inputs_to(zl, y, 0, block):
-                copy.wait_recv()
-
+            drain(arecv.at[0, block], 6 * TOK, TOK)
+            inputs_to(zl, y, block)[4].wait_recv()
+
+        if block == 1:
+            h_across(2, ctx).start()
+            h_across(3, ctx).start()
+            h_start(2, 0)
+            h_start(3, 0)
         if block == 5:
             h_forward(0, 0)
             h_forward(1, 0)
@@ -310,94 +298,127 @@
     for block in range(CTX - SPAN, CTX):
         finish_keys(block)
 
+    for src, dst in out_refs(ctx):
+        pltpu.make_async_copy(src, dst, lsem.at[0]).start()
+
     def columns(kind):
         return jnp.concatenate([g4[2 * kind], g4[2 * kind + 1]], axis=1)
 
     far_core = (core + 1) % NC
 
-    def core_copy(block):
+    def part_rows(part):
+        return ((0, split), (split, xrows - split))[part]
+
+    def core_copy(part, step):
+        piece = (x_of(step), pl.ds(*part_rows(part)))
         return remote(
-            csend.at[block], crecv.at[block], csem.at[block], crsem.at[block],
+            csend.at[piece], crecv.at[piece], csem.at[0], crsem.at[step, part],
             place(x, zh, far_core, zl, y),
         )
 
-    def x_copy(step, block):
+    def x_copy(part, step, nx):
+        piece = (step, pl.ds(*part_rows(part)))
         return remote(
-            xsend.at[step], xrecv.at[step], xsem.at[step], xrsem.at[step],
-            place(block, zh, core, zl, y),
-        )
-
-    def weights_far(step):
-        block = (x + step + 1) % NX
-        h_arrive(step)
-        if step == 0:
+            xsend.at[piece], xrecv.at[piece], xsem.at[0], xrsem.at[part],
+            place(nx, zh, core, zl, y),
+        )
+
+    def weights_far(part, step):
+        if part == 0:
+            h_arrive(step)
+        if part == 0 and step == 0:
             h_own.wait()
-            for block_in in range(CTX):
-                for copy in trade(block_in, False):
-                    copy.wait_recv()
-        csend[block] = dot(hall[at(block, xrows), :], columns(far_core)).astype(BF16)
-        core_copy(block).start()
-
-    def weights_own(step):
-        block = (x + step + 1) % NX
-        wown[...] = dot(hall[at(block, xrows), :], columns(core))
-        core_copy(block).wait_recv()
+            drain(grecv.at[0], CTX * TOK, 2 * TOK)
+        csend[x_of(step), pl.ds(*part_rows(part)), :] = dot(
+            hall[h_rows(step, part), :], columns(far_core)
+        ).astype(BF16)
+        core_copy(part, step).start()
+
+    def weights_own(part, step):
+        rows = pl.ds(*part_rows(part))
+        mine = dot(hall[h_rows(step, part), :], columns(core))
+        core_copy(part, step).wait_recv()
+        total = mine + crecv[x_of(step), rows, :].astype(F32)
         if step < NX - 1:
-            xsend[step] = (wown[...] + crecv[block].astype(F32)).astype(BF16)
-            x_copy(step, block).start()
+            xsend[step, rows, :] = total.astype(BF16)
+            x_copy(part, step, x_of(step)).start()
         else:
-            tsum[:xrows, :] = wown[...] + crecv[block].astype(F32)
-
-    def give_back():
-        for block in range(CTX):
-            for index in range(3):
-                start_out(index, block)
-
+            tsum[rows, :] = total
+
+    def x_finish(part):
+        rows = pl.ds(*part_rows(part))
+        drain(xrsem.at[part], (NX - 1) * part_rows(part)[1], 2 * HD)
+        tsum[rows, :] += (
+            xrecv[0, rows, :].astype(F32) + xrecv[1, rows, :].astype(F32)
+            + xrecv[2, rows, :].astype(F32)
+        )
+        for piece in (2 * part, 2 * part + 1):
+            zsend[piece] = tsum[piece * frows : piece * frows + zrows, :].astype(BF16)
+
+            @pl.when(z_mine(piece))
+            def _():
+                z_near(piece).start()
+
+            @pl.when(jnp.logical_not(z_mine(piece)))
+            def _():
+                z_far(piece).start()
+
+    def z_mine(piece):
+        return (2 * zl + piece // 2 == zh) & (piece % 2 == core) & (core == zl)
+
+    def z_far(piece):
+        return remote(
+            zsend.at[piece], zrecv.at[zh], zsem.at[piece], zrsem.at[zh],
+            place(x, 2 * zl + piece // 2, piece % 2, core, y),
+        )
+
+    def z_near(piece):
+        return pltpu.make_async_copy(zsend.at[piece], zrecv.at[zh], zsem.at[piece])
+
+    def give_back(peers):
+        for dl, dy in peers:
+            block = (zl + dl) % 2 * NY + (y + dy) % NY
+            for src, dst in out_refs(block):
+                remote(src, dst, osend.at[0], orecv.at[0], (dp, block)).start()
+
+    tsum[xrows:, :] = jnp.zeros((tsum.shape[0] - xrows, tsum.shape[1]), F32)
     h_forward(2, 0)
     h_forward(3, 0)
     h_forward(0, 1)
     h_forward(1, 1)
     h_forward(2, 1)
-    weights_far(0)
+    weights_far(0, 0)
     h_forward(3, 1)
-    weights_far(1)
-    weights_own(0)
-    give_back()
-    weights_far(2)
-    weights_own(1)
-    weights_far(3)
-    weights_own(2)
-    weights_own(3)
-
-    for step in range(NX - 1):
-        x_copy(step, x).wait_recv()
-    tsum[:xrows, :] += (
-        xrecv[0].astype(F32) + xrecv[1].astype(F32) + xrecv[2].astype(F32)
-    )
-    tsum[xrows:, :] = jnp.zeros((tsum.shape[0] - xrows, tsum.shape[1]), F32)
-
-    def z_mine(piece):
-        return (2 * zl + piece // 2 == zh) & (piece % 2 == core) & (core == zl)
-
-    def z_far(piece):
-        return remote(
-            zsend.at[piece], zrecv.at[zh], zsem.at[piece], zrsem.at[zh],
-            place(x, 2 * zl + piece // 2, piece % 2, core, y),
-        )
-
-    def z_near(piece):
-        return pltpu.make_async_copy(zsend.at[piece], zrecv.at[zh], zsem.at[piece])
-
-    for piece in range(4):
-        zsend[piece] = tsum[piece * frows : piece * frows + zrows, :].astype(BF16)
-
-        @pl.when(z_mine(piece))
-        def _():
-            z_near(piece).start()
-
-        @pl.when(jnp.logical_not(z_mine(piece)))
-        def _():
-            z_far(piece).start()
+    weights_far(0, 1)
+    weights_own(0, 0)
+    give_back(PEERS)
+    weights_far(0, 2)
+    weights_own(0, 1)
+    weights_far(0, 3)
+    weights_own(0, 2)
+    weights_own(0, 3)
+    weights_far(1, 0)
+    weights_far(1, 1)
+    weights_own(1, 0)
+    weights_far(1, 2)
+    weights_own(1, 1)
+    weights_far(1, 3)
+    weights_own(1, 2)
+    weights_own(1, 3)
+
+    x_finish(0)
+    x_finish(1)
+
+    drain(asend.at[0], half, 4 * TOK)
+    for copy in input_copies[4::5]:
+        copy.wait_send()
+    drain(hsend.at[0], half, 7 * TOK)
+    drain(gsend.at[0], CTX * TOK, 2 * TOK)
+    drain(csem.at[0], half, 2 * HD)
+    drain(xsem.at[0], (NX - 1) * xrows, 2 * HD)
+    drain(lsem.at[0], 4 * TOK, TOK)
+    drain(osend.at[0], (CTX - 1) * TOK, 4 * TOK)
+    drain(orecv.at[0], (CTX - 1) * TOK, 4 * TOK)
 
     for piece in range(4):
         @pl.when(z_mine(piece))
@@ -422,44 +443,6 @@
         (zrecv[0, :frows, :].astype(F32) + zrecv[1, :frows, :].astype(F32))
         + (zrecv[2, :frows, :].astype(F32) + zrecv[3, :frows, :].astype(F32))
     )
-
-    for block in range(CTX):
-        for index in range(3):
-            @pl.when(ctx != block)
-            def _():
-                out_far(index, block).wait_send()
-
-            @pl.when(ctx == block)
-            def _():
-                out_near(index, block).wait()
-
-        for copy in trade(block, True):
-            copy.wait_send()
-    for block in range(CTX):
-        from_head = 2 * (block % NY) + block // NY
-        rows = pl.ds(0, TOK)
-
-        @pl.when(ctx != block)
-        def _():
-            for index, (src, dst) in enumerate((
-                (dqs.at[rows, :], dq_out.at[:, at(from_head, 2 * HD)]),
-                (g4.at[0, rows, :], dk_out.at[:, at(from_head, HD)]),
-                (g4.at[0, rows, :], dv_out.at[:, at(from_head, HD)]),
-            )):
-                remote(src, dst, osend.at[index, 0], orecv.at[index, block], (dp, partner)).wait_recv()
-
-    for copy in input_copies:
-        copy.wait_send()
-    for step in range(NX):
-        h_across(step, ctx).wait_send()
-        for kind in range(2):
-            for way in range(2):
-                h_step(step, kind, way, y).wait_send()
-                h_pass(step, kind, way, y - 1 + 2 * way).wait_send()
-    for step in range(1, NX + 1):
-        core_copy((x + step) % NX).wait_send()
-    for step in range(NX - 1):
-        x_copy(step, x).wait_send()
 
 
 def hand_over(*refs):
@@ -507,7 +490,6 @@
         pltpu.VMEM((seq, HD), F32),
         pltpu.VMEM((2, half, TOK), BF16),
         pltpu.VMEM((half, seq), BF16),
-        pltpu.VMEM((xrows, 2 * HD), F32),
         pltpu.VMEM((NX, xrows, 2 * HD), BF16),
         pltpu.VMEM((NX, xrows, 2 * HD), BF16),
         pltpu.VMEM((NX - 1, xrows, 2 * HD), BF16),
@@ -516,14 +498,12 @@
         pltpu.VMEM((4, zrows, 2 * HD), BF16),
         pltpu.VMEM((NZ, zrows, 2 * HD), BF16),
         dma((7,)),
-        dma((5, 7)), dma((5, CTX)),
-        dma((3, CTX)), dma((3, CTX)),
-        dma((2, CTX)), dma((2, CTX)),
-        dma((NX,)), dma((NX,)),
-        dma((NX, 2, 2)), dma((NX, 2, 2)),
-        dma((NX, 2, 2)), dma((NX, 2, 2)),
-        dma((NX,)), dma((NX,)),
-        dma((NX - 1,)), dma((NX - 1,)),
+        dma((8,)), dma((2, CTX)),
+        dma((1,)), dma((1,)),
+        dma((1,)), dma((1,)),
+        dma((1,)), dma((NX,)), dma((NX, 2)), dma((NX,)),
+        dma((1,)), dma((NX, 2)),
+        dma((1,)), dma((2,)),
         dma((4,)), dma((NZ,)),
     ]
     outs = (

time: 75.5 us -> 73.4 us (0.972)
  Pallas kernels: 74.8 us -> 72.7 us
    pallas_call x1, Pallas kernels: 72.7 us -> 70.6 us  [local(): pl.pallas_call(kernel, out_shape=outs, in_specs=[any_spec] * 6, out_specs...]
where the time goes in v3:
time: 73.4 us; the launch traced here: 73.3 us
  Pallas kernels  72.7 us (99%)
    pallas_call x1, Pallas kernels, local(): pl.pallas_call(kernel, out_shape=outs, in_specs=[any_spec] * 6, out_specs...  70.6 us
    pallas_call x1, Pallas kernels, local(): pl.pallas_call(hand_over, out_shape=outs, in_specs=[any_spec] * 4, out_sp...  2.09 us

profile of v3, /device:TPU:1, one launch (start us, length us, event | category | flops | bytes accessed | tf_op | source)
XLA Modules:
  0.0 73.3 jit_solution(13548038502643947331)
XLA Ops:
  0.6 70.6 %shard_map.93 = (bf16[128,2048]{1,0:T(8,128)(2,1)}, bf16[128,1024]{1,0:T(8,128)(2,1)}, bf16[128,1024]{1,0:T(8,128)(2,1)}, f32[84,256]{1,0:T(8,128)}) custom-call(bf16[128,2688]{1,0:T(8,128)(2,1)} %bitcast.8, bf16[128,2048]{1,0:T(8,128)(2,1)} %bitcast.9, bf16[128,1024]{1,0:T(8,128)(2,1)} %bitcast.11, bf16[128,1024]{1,0:T(8,128)(2,1)} %bitcast.12, ...), custom_call_target="tpu_custom_call" | custom-call | tf_op jit(solution)/shard_map/pallas_call | solution.py:515
  71.2 2.1 %shard_map.94 = (bf16[128,2048]{1,0:T(8,128)(2,1)}, bf16[128,1024]{1,0:T(8,128)(2,1)}, bf16[128,1024]{1,0:T(8,128)(2,1)}, f32[84,256]{1,0:T(8,128)}) custom-call(bf16[128,2048]{1,0:T(8,128)(2,1)} %get-tuple-element.12.refs_0_, bf16[128,1024]{1,0:T(8,128)(2,1)} %get-tuple-element.13.refs_1_, bf16[128,1024]{1,0:T(8,128)(2,1)} %get-tuple-element.14.refs_2_, ...), custom_call_target="tpu_custom_call" | custom-call | tf_op jit(solution)/shard_map/pallas_call | solution.py:525

commit v4 on v3

--- a/solution.py
+++ b/solution.py
@@ -386,12 +386,13 @@
     h_forward(3, 0)
     h_forward(0, 1)
     h_forward(1, 1)
+    give_back(PEERS[6:])
     h_forward(2, 1)
     weights_far(0, 0)
     h_forward(3, 1)
     weights_far(0, 1)
     weights_own(0, 0)
-    give_back(PEERS)
+    give_back(PEERS[:6])
     weights_far(0, 2)
     weights_own(0, 1)
     weights_far(0, 3)
@@ -448,13 +449,20 @@
 def hand_over(*refs):
     sources, targets, stages = refs[:4], refs[4:8], refs[8:12]
     sems = refs[12]
+    pieces = [
+        (index, pl.ds(piece * 32, 32)) for piece in range(TOK // 32) for index in range(3)
+    ] + [(3, pl.ds(0, refs[3].shape[0]))]
     loads = [
-        pltpu.make_async_copy(src, stage, sems.at[0, index])
-        for index, (src, stage) in enumerate(zip(sources, stages))
+        pltpu.make_async_copy(
+            sources[index].at[rows, :], stages[index].at[rows, :], sems.at[0, number]
+        )
+        for number, (index, rows) in enumerate(pieces)
     ]
     stores = [
-        pltpu.make_async_copy(stage, dst, sems.at[1, index])
-        for index, (stage, dst) in enumerate(zip(stages, targets))
+        pltpu.make_async_copy(
+            stages[index].at[rows, :], targets[index].at[rows, :], sems.at[1, number]
+        )
+        for number, (index, rows) in enumerate(pieces)
     ]
     for copy in loads:
         copy.start()
@@ -527,7 +535,7 @@
         out_shape=outs,
         in_specs=[any_spec] * 4,
         out_specs=(any_spec,) * 4,
-        scratch_shapes=[pltpu.VMEM(out.shape, out.dtype) for out in outs] + [dma((2, 4))],
+        scratch_shapes=[pltpu.VMEM(out.shape, out.dtype) for out in outs] + [dma((2, 13))],
     )(*parts)
     return dq[None], dk[None], dv[None], dw
 

time: 73.4 us -> 70.7 us (0.963)
  Pallas kernels: 72.7 us -> 70 us
    pallas_call x1, Pallas kernels: 70.6 us -> 67.8 us  [local(): pl.pallas_call(kernel, out_shape=outs, in_specs=[any_spec] * 6, out_specs...]
where the time goes in v4:
time: 70.7 us; the launch traced here: 70.6 us
  Pallas kernels  70 us (99%)
    pallas_call x1, Pallas kernels, local(): pl.pallas_call(kernel, out_shape=outs, in_specs=[any_spec] * 6, out_specs...  67.8 us
    pallas_call x1, Pallas kernels, local(): pl.pallas_call(hand_over, out_shape=outs, in_specs=[any_spec] * 4, out_sp...  2.2 us

profile of v4, /device:TPU:1, one launch (start us, length us, event | category | flops | bytes accessed | tf_op | source)
XLA Modules:
  0.0 70.6 jit_solution(8734470181710260300)
XLA Ops:
  0.6 67.8 %shard_map.93 = (bf16[128,2048]{1,0:T(8,128)(2,1)}, bf16[128,1024]{1,0:T(8,128)(2,1)}, bf16[128,1024]{1,0:T(8,128)(2,1)}, f32[84,256]{1,0:T(8,128)}) custom-call(bf16[128,2688]{1,0:T(8,128)(2,1)} %bitcast.8, bf16[128,2048]{1,0:T(8,128)(2,1)} %bitcast.9, bf16[128,1024]{1,0:T(8,128)(2,1)} %bitcast.11, bf16[128,1024]{1,0:T(8,128)(2,1)} %bitcast.12, ...), custom_call_target="tpu_custom_call" | custom-call | tf_op jit(solution)/shard_map/pallas_call | solution.py:523
  68.4 2.2 %shard_map.94 = (bf16[128,2048]{1,0:T(8,128)(2,1)}, bf16[128,1024]{1,0:T(8,128)(2,1)}, bf16[128,1024]{1,0:T(8,128)(2,1)}, f32[84,256]{1,0:T(8,128)}) custom-call(bf16[128,2048]{1,0:T(8,128)(2,1)} %get-tuple-element.12.refs_0_, bf16[128,1024]{1,0:T(8,128)(2,1)} %get-tuple-element.13.refs_1_, bf16[128,1024]{1,0:T(8,128)(2,1)} %get-tuple-element.14.refs_2_, ...), custom_call_target="tpu_custom_call" | custom-call | tf_op jit(solution)/shard_map/pallas_call | solution.py:533

commit v5 on v4

--- a/solution.py
+++ b/solution.py
@@ -392,11 +392,12 @@
     h_forward(3, 1)
     weights_far(0, 1)
     weights_own(0, 0)
-    give_back(PEERS[:6])
+    give_back(PEERS[:3])
     weights_far(0, 2)
     weights_own(0, 1)
     weights_far(0, 3)
     weights_own(0, 2)
+    give_back(PEERS[3:6])
     weights_own(0, 3)
     weights_far(1, 0)
     weights_far(1, 1)

time: 70.7 us -> 70.7 us (level)
  no operation moved by 1% of the time
where the time goes in v5:
time: 70.7 us; the launch traced here: 70.6 us
  Pallas kernels  70 us (99%)
    pallas_call x1, Pallas kernels, local(): pl.pallas_call(kernel, out_shape=outs, in_specs=[any_spec] * 6, out_specs...  67.7 us
    pallas_call x1, Pallas kernels, local(): pl.pallas_call(hand_over, out_shape=outs, in_specs=[any_spec] * 4, out_sp...  2.2 us

profile of v5, /device:TPU:1, one launch (start us, length us, event | category | flops | bytes accessed | tf_op | source)
XLA Modules:
  0.0 70.6 jit_solution(2718369446280212443)
XLA Ops:
  0.6 67.7 %shard_map.93 = (bf16[128,2048]{1,0:T(8,128)(2,1)}, bf16[128,1024]{1,0:T(8,128)(2,1)}, bf16[128,1024]{1,0:T(8,128)(2,1)}, f32[84,256]{1,0:T(8,128)}) custom-call(bf16[128,2688]{1,0:T(8,128)(2,1)} %bitcast.8, bf16[128,2048]{1,0:T(8,128)(2,1)} %bitcast.9, bf16[128,1024]{1,0:T(8,128)(2,1)} %bitcast.11, bf16[128,1024]{1,0:T(8,128)(2,1)} %bitcast.12, ...), custom_call_target="tpu_custom_call" | custom-call | tf_op jit(solution)/shard_map/pallas_call | solution.py:524
  68.4 2.2 %shard_map.94 = (bf16[128,2048]{1,0:T(8,128)(2,1)}, bf16[128,1024]{1,0:T(8,128)(2,1)}, bf16[128,1024]{1,0:T(8,128)(2,1)}, f32[84,256]{1,0:T(8,128)}) custom-call(bf16[128,2048]{1,0:T(8,128)(2,1)} %get-tuple-element.12.refs_0_, bf16[128,1024]{1,0:T(8,128)(2,1)} %get-tuple-element.13.refs_1_, bf16[128,1024]{1,0:T(8,128)(2,1)} %get-tuple-element.14.refs_2_, ...), custom_call_target="tpu_custom_call" | custom-call | tf_op jit(solution)/shard_map/pallas_call | solution.py:534
